TPU v7x, 256 devices: a whole 4x4x8 slice. The times are simulated.
256 devices in a mesh: section: 8 (over y, core), rows: 32 (over x, z).
Axes of the slice: x: 4, y: 4, z: 8, core: 2. Of those that a mesh axis runs over, the one named last changes fastest.
Arguments:
- grad_in: bfloat16 [8, 8192, 256], P('section', 'rows'), may hold values from -6 to 6
- grad_last: bfloat16 [8192, 256], P('rows'), may hold values from -6 to 6
- support: bfloat16 [8, 2, 2, 8192, 256], P('section', None, None, 'rows'), may hold values from -6 to 6
- preact: bfloat16 [8, 2, 2, 8192, 256], P('section', None, None, 'rows'), may hold values from -6 to 6
- weights: bfloat16 [8, 2, 256, 256], P('section'), may hold values from -0.375 to 0.375
- tile_vals: bfloat16 [8, 2, 3072, 128, 128], P('section', None, 'rows'), may hold values from -0.078125 to 0.078125
- tile_row: int32 [8, 2, 3072], P('section', None, 'rows'), may hold values from 0 to 1
- tile_col: int32 [8, 2, 3072], P('section', None, 'rows'), may hold values from 0 to 63, as said below
- tile_count: int32 [8, 2, 32], P('section', None, 'rows'), may hold values from 48 to 96, as said below
Outputs:
- handoff: bfloat16 [2, 8, 8192, 256], P(None, 'section', 'rows')
- init_grad: float32 [8, 2, 8192, 256], P('section', None, 'rows')
- weight_grad: float32 [8, 2, 256, 256], P('section')
Inputs may be any that keep to these rules, and one draw needn't show every extreme that they name: tile_count[s, t, d] is the number of live entries in device d's list; in every section and micro-batch some device has all 96 live. `tile_col`: for every section, micro-batch and pair of devices d and o with o != d, all entries of device d's list (live or padding) whose column tile lies in device o's rows name one and the same of o's 2 row tiles.
All inputs are finite; a program needn't handle non-finite values.
Results may differ from a plain program's by a relative error of at most 0.0066.
Values may be sent and summed in bfloat16 or wider, within the bound.
A program may use at most 128 MiB of HBM per device.

v0:
```python
import jax
import jax.numpy as jnp
from jax import lax
from jax.sharding import PartitionSpec as P

ALPHA = 0.1
BETA_SCALE = 0.5


def passed_along(block, axis, distance):
    devices = range(lax.axis_size(axis))
    route = [(i - distance, i) for i in devices if i - distance in devices]
    return lax.ppermute(block, axis, route)


def tile_product(gathered, values, row_local, index, count, row_tiles):
    tile = values.shape[-1]
    width = gathered.shape[-1]
    blocks = gathered.reshape(-1, tile, width)[index]
    products = jnp.einsum("kab,kbf->kaf", values, blocks, preferred_element_type=jnp.float32)
    live = jnp.arange(index.shape[0]) < count
    select = ((row_local[None, :] == jnp.arange(row_tiles)[:, None]) & live[None, :]).astype(
        jnp.float32
    )
    summed = jnp.einsum("ik,kaf->iaf", select, products, precision=lax.Precision.HIGHEST)
    return summed.reshape(row_tiles * tile, width)


def shards(grad_in, grad_last, support, preact, weights, tile_vals, tile_row, tile_col, tile_count):
    section = lax.axis_index("section")
    sections = lax.axis_size("section")
    ticks = support.shape[1]
    layers = support.shape[2]
    rows_dev, width = grad_last.shape
    tile = tile_vals.shape[-1]
    row_tiles = rows_dev // tile
    weight_acc = [jnp.zeros((width, width), jnp.float32) for layer in range(layers)]
    handed = []
    initial = []
    for tick in range(ticks):
        if tick == 0:
            grad = grad_in[0]
        else:
            passed = passed_along(handed[-1], "section", -1)
            grad = jnp.where(section == sections - 1, grad_last, passed)
        columns = tile_col[0, tick]
        count = tile_count[0, tick, 0]
        toward = jnp.zeros((rows_dev, width), jnp.float32)
        for layer in reversed(range(layers)):
            beta = jnp.log(BETA_SCALE / (layers * section + layer + 1).astype(jnp.float32) + 1.0)
            weight = weights[0, layer]
            masked = jnp.where(preact[0, tick, layer] > 0, grad, jnp.zeros_like(grad))
            term = beta * jnp.dot(
                support[0, tick, layer].T, masked, preferred_element_type=jnp.float32
            )
            weight_acc[layer] = weight_acc[layer] + lax.psum(term, "rows")
            image = (
                (1.0 - beta) * masked.astype(jnp.float32)
                + beta * jnp.dot(masked, weight.T, preferred_element_type=jnp.float32)
            ).astype(jnp.bfloat16)
            toward = toward + ALPHA * image.astype(jnp.float32)
            gathered = lax.all_gather(image, "rows", axis=0, tiled=True)
            spread = tile_product(
                gathered, tile_vals[0, tick], tile_row[0, tick], columns, count, row_tiles
            )
            grad = ((1.0 - ALPHA) * spread).astype(jnp.bfloat16)
        handed.append(grad)
        initial.append(toward)
    return (jnp.stack(handed)[:, None], jnp.stack(initial)[None], jnp.stack(weight_acc)[None])


def solution(mesh):
    return jax.shard_map(
        shards,
        mesh=mesh,
        in_specs=(
            P("section", "rows", None),
            P("rows", None),
            P("section", None, None, "rows", None),
            P("section", None, None, "rows", None),
            P("section", None, None, None),
            P("section", None, "rows", None, None),
            P("section", None, "rows"),
            P("section", None, "rows"),
            P("section", None, "rows"),
        ),
        out_specs=(
            P(None, "section", "rows", None),
            P("section", None, "rows", None),
            P("section", None, None, None),
        ),
        check_vma=False,
    )
```

profile of v0, /device:TPU:1, one launch (start us, length us, event | category | flops | bytes accessed | tf_op | source)
XLA Modules:
  0.0 646.6 jit_solution(17739819495514293798)
XLA Ops:
  7.3 2.1 fusion.15
  9.5 1.3 fusion.83
  13.0 81.1 %all-gather.5.cloned.1.call-done = bf16[8192,256]{1,0:T(8,128)(2,1)} async-done(((bf16[256,256]{1,0:T(8,128)(2,1)}), bf16[8192,256]{1,0:T(8,128)(2,1)}) %all-gather.5.cloned.1.call-update) | async-done | bytes 4194320 | tf_op jit(solution)/shard_map/all_gather | solution.py:62
  94.1 8.1 %gather_fusion = bf16[96,128,256]{2,1,0:T(8,128)(2,1)} fusion(bf16[64,128,256]{2,1,0:T(8,128)(2,1)} %bitcast.141, s32[1024]{0:T(1024)S(1)} %pad_clamp_fusion.1), kind=kCustom, calls=%fused_computation | custom fusion | bytes 12583296 | tf_op jit(solution)/shard_map/gather | solution.py:19
  102.2 10.1 %convolution_bitcast_fusion.3 = f32[96,128,256]{1,2,0:T(8,128)} fusion(bf16[96,128,256]{2,1,0:T(8,128)(2,1)} %gather_fusion, bf16[1,2,96,128,128]{4,3,2,1,0:T(8,128)(2,1)} %param.14), kind=kOutput, calls=%fused_computation.7 | convolution fusion | flops 805306368 | bytes 22020096 | tf_op jit(solution)/shard_map/kab,kbf->kaf/dot_general | solution.py:20
  112.2 12.8 %copy.38 = f32[96,128,256]{2,0,1:T(8,128)} copy(f32[96,128,256]{1,2,0:T(8,128)} %convolution_bitcast_fusion.3) | data formatting | bytes 25165824 | tf_op jit(solution)/shard_map/kab,kbf->kaf/dot_general | solution.py:20
  125.0 7.1 %fusion.65 = f32[2,128,256]{2,0,1:T(2,128)S(1)} fusion(f32[96,128,256]{2,0,1:T(8,128)} %copy.38, pred[96]{0:T(512)(128)(4,1)S(1)} %iota_compare_fusion.1, s32[96]{0:T(128)S(1)} %get-tuple-element.18), kind=kOutput, calls=%fused_computation.97 | convolution fusion | flops 75497856 | bytes 12845536 | tf_op jit(solution)/shard_map/ik,kaf->iaf/dot_general | solution.py:25
  132.1 0.9 fusion.16
  133.3 78.9 %all-gather.7.cloned.1.call-done = bf16[8192,256]{1,0:T(8,128)(2,1)} async-done(((bf16[256,256]{1,0:T(8,128)(2,1)}), bf16[8192,256]{1,0:T(8,128)(2,1)}) %all-gather.7.cloned.1.call-update) | async-done | bytes 4194320 | tf_op jit(solution)/shard_map/all_gather | solution.py:62
  212.2 8.1 %gather_fusion.1 = bf16[96,128,256]{2,1,0:T(8,128)(2,1)} fusion(bf16[64,128,256]{2,1,0:T(8,128)(2,1)} %bitcast.144, s32[1024]{0:T(1024)S(1)} %pad_clamp_fusion.1), kind=kCustom, calls=%fused_computation.1 | custom fusion | bytes 12583296 | tf_op jit(solution)/shard_map/gather | solution.py:19
  220.3 10.1 %convolution_bitcast_fusion.2 = f32[96,128,256]{1,2,0:T(8,128)} fusion(bf16[96,128,256]{2,1,0:T(8,128)(2,1)} %gather_fusion.1, bf16[1,2,96,128,128]{4,3,2,1,0:T(8,128)(2,1)} %param.14), kind=kOutput, calls=%fused_computation.6 | convolution fusion | flops 805306368 | bytes 22020096 | tf_op jit(solution)/shard_map/kab,kbf->kaf/dot_general | solution.py:20
  230.3 12.8 %copy.41 = f32[96,128,256]{2,0,1:T(8,128)} copy(f32[96,128,256]{1,2,0:T(8,128)} %convolution_bitcast_fusion.2) | data formatting | bytes 25165824 | tf_op jit(solution)/shard_map/kab,kbf->kaf/dot_general | solution.py:20
  243.1 7.1 %fusion.63 = f32[2,128,256]{2,0,1:T(2,128)S(1)} fusion(f32[96,128,256]{2,0,1:T(8,128)} %copy.41, pred[96]{0:T(512)(128)(4,1)S(1)} %iota_compare_fusion.1, s32[96]{0:T(128)S(1)} %get-tuple-element.18), kind=kOutput, calls=%fused_computation.95 | convolution fusion | flops 75497856 | bytes 12845536 | tf_op jit(solution)/shard_map/ik,kaf->iaf/dot_general | solution.py:25
  250.2 5.2 collective-permute-start
  255.4 3.7 collective-permute-done
  261.5 0.9 fusion.9
  262.4 73.5 %all-gather.9.cloned.1.call-done = bf16[8192,256]{1,0:T(8,128)(2,1)} async-done(((bf16[256,256]{1,0:T(8,128)(2,1)}), bf16[8192,256]{1,0:T(8,128)(2,1)}) %all-gather.9.cloned.1.call-update) | async-done | bytes 4194320 | tf_op jit(solution)/shard_map/all_gather | solution.py:62
  336.0 8.1 %gather_fusion.2 = bf16[96,128,256]{2,1,0:T(8,128)(2,1)} fusion(bf16[64,128,256]{2,1,0:T(8,128)(2,1)} %bitcast.143, s32[1024]{0:T(1024)S(1)} %pad_clamp_fusion), kind=kCustom, calls=%fused_computation.2 | custom fusion | bytes 12583296 | tf_op jit(solution)/shard_map/gather | solution.py:19
  344.1 10.1 %convolution_bitcast_fusion.1 = f32[96,128,256]{1,2,0:T(8,128)} fusion(bf16[96,128,256]{2,1,0:T(8,128)(2,1)} %gather_fusion.2, bf16[1,2,96,128,128]{4,3,2,1,0:T(8,128)(2,1)} %param.14), kind=kOutput, calls=%fused_computation.5 | convolution fusion | flops 805306368 | bytes 22020096 | tf_op jit(solution)/shard_map/kab,kbf->kaf/dot_general | solution.py:20
  354.1 12.8 %copy.44 = f32[96,128,256]{2,0,1:T(8,128)} copy(f32[96,128,256]{1,2,0:T(8,128)} %convolution_bitcast_fusion.1) | data formatting | bytes 25165824 | tf_op jit(solution)/shard_map/kab,kbf->kaf/dot_general | solution.py:20
  366.9 7.0 %fusion.61 = f32[2,128,256]{2,0,1:T(2,128)S(1)} fusion(f32[96,128,256]{2,0,1:T(8,128)} %copy.44, pred[96]{0:T(512)(128)(4,1)S(1)} %iota_compare_fusion, s32[96]{0:T(128)S(1)} %get-tuple-element.17), kind=kOutput, calls=%fused_computation.93 | convolution fusion | flops 75497856 | bytes 12845536 | tf_op jit(solution)/shard_map/ik,kaf->iaf/dot_general | solution.py:25
  374.0 0.9 fusion.11
  375.3 0.9 fusion.17
  376.2 0.9 multiply_bitcast_fusion
  378.0 139.9 %all-reduce.3.cloned.1.call-done = (f32[256,256]{0,1:T(8,128)}, f32[256,256]{0,1:T(8,128)}) async-done(((f32[256,256]{0,1:T(8,128)}, f32[256,256]{0,1:T(8,128)}), (f32[256,256]{0,1:T(8,128)}, f32[256,256]{0,1:T(8,128)})) %all-reduce.3.cloned.1.call-update) | async-done | bytes 524304 | tf_op jit(solution)/shard_map/psum | solution.py:56
  518.0 1.1 maximum_bitcast_fusion.1
  519.0 1.0 copy.50
  520.0 81.3 %all-gather.11.cloned.1.call-done = bf16[8192,256]{1,0:T(8,128)(2,1)} async-done(((bf16[256,256]{1,0:T(8,128)(2,1)}), bf16[8192,256]{1,0:T(8,128)(2,1)}) %all-gather.11.cloned.1.call-update) | async-done | bytes 4194320 | tf_op jit(solution)/shard_map/all_gather | solution.py:62
  601.3 8.1 %gather_fusion.3 = bf16[96,128,256]{2,1,0:T(8,128)(2,1)} fusion(bf16[64,128,256]{2,1,0:T(8,128)(2,1)} %bitcast.142, s32[1024]{0:T(1024)S(1)} %pad_clamp_fusion), kind=kCustom, calls=%fused_computation.3 | custom fusion | bytes 12583296 | tf_op jit(solution)/shard_map/gather | solution.py:19
  609.4 10.1 %convolution_bitcast_fusion = f32[96,128,256]{1,2,0:T(8,128)} fusion(bf16[96,128,256]{2,1,0:T(8,128)(2,1)} %gather_fusion.3, bf16[1,2,96,128,128]{4,3,2,1,0:T(8,128)(2,1)} %param.14), kind=kOutput, calls=%fused_computation.4 | convolution fusion | flops 805306368 | bytes 22020096 | tf_op jit(solution)/shard_map/kab,kbf->kaf/dot_general | solution.py:20
  619.5 12.8 %copy.47 = f32[96,128,256]{2,0,1:T(8,128)} copy(f32[96,128,256]{1,2,0:T(8,128)} %convolution_bitcast_fusion) | data formatting | bytes 25165824 | tf_op jit(solution)/shard_map/kab,kbf->kaf/dot_general | solution.py:20
  632.3 7.0 %fusion.59 = f32[2,128,256]{2,0,1:T(2,128)S(1)} fusion(f32[96,128,256]{2,0,1:T(8,128)} %copy.47, pred[96]{0:T(512)(128)(4,1)S(1)} %iota_compare_fusion, s32[96]{0:T(128)S(1)} %get-tuple-element.17), kind=kOutput, calls=%fused_computation.91 | convolution fusion | flops 75497856 | bytes 12845536 | tf_op jit(solution)/shard_map/ik,kaf->iaf/dot_general | solution.py:25
  (43 shorter events, 6.9 us)
Async XLA Ops:
  7.2 86.9 %all-gather.5.cloned.1.call-start = ((), (), s32[]{:S(2)}) async-start(), calls=%async_computation | async-start | bytes 4325376 | tf_op jit(solution)/shard_map/all_gather | solution.py:62
  9.4 202.8 %all-gather.7.cloned.1.call-start = ((), (), s32[]{:S(2)}) async-start(), calls=%async_computation.1 | async-start | bytes 4325376 | tf_op jit(solution)/shard_map/all_gather | solution.py:62
  125.0 7.1 %copy-start = (bf16[1,2,2,256,256]{4,3,2,1,0:T(8,128)(2,1)S(1)}, bf16[1,2,2,256,256]{4,3,2,1,0:T(8,128)(2,1)}, u32[]{:S(2)}) copy-start(bf16[1,2,2,256,256]{4,3,2,1,0:T(8,128)(2,1)} %param.12) | copy-start | bytes 1572868
  125.0 7.1 %copy-start.7 = (bf16[1,2,256,256]{3,2,1,0:T(8,128)(2,1)S(1)}, bf16[1,2,256,256]{3,2,1,0:T(8,128)(2,1)}, u32[]{:S(2)}) copy-start(bf16[1,2,256,256]{3,2,1,0:T(8,128)(2,1)} %param.13) | copy-start | bytes 786436
  133.0 202.9 %all-gather.9.cloned.1.call-start = ((), (), s32[]{:S(2)}) async-start(), calls=%async_computation.2 | async-start | bytes 4325376 | tf_op jit(solution)/shard_map/all_gather | solution.py:62
  243.1 16.1 %copy-start.5 = (bf16[256,256]{1,0:T(8,128)(2,1)S(1)}, bf16[256,256]{1,0:T(8,128)(2,1)}, u32[]{:S(2)}) copy-start(bf16[256,256]{1,0:T(8,128)(2,1)} %param.10) | copy-start | bytes 393220
  243.1 17.9 %copy-start.1 = (bf16[1,2,2,256,256]{4,3,2,1,0:T(8,128)(2,1)S(1)}, bf16[1,2,2,256,256]{4,3,2,1,0:T(8,128)(2,1)}, u32[]{:S(2)}) copy-start(bf16[1,2,2,256,256]{4,3,2,1,0:T(8,128)(2,1)} %param.11) | copy-start | bytes 1572868
  243.1 17.9 %copy-start.6 = (bf16[1,256,256]{2,1,0:T(8,128)(2,1)S(1)}, bf16[1,256,256]{2,1,0:T(8,128)(2,1)}, u32[]{:S(2)}) copy-start(bf16[1,256,256]{2,1,0:T(8,128)(2,1)} %param.9) | copy-start | bytes 393220
  250.2 8.9 %collective-permute-start = (bf16[256,256]{1,0:T(8,128)(2,1)S(1)}, bf16[256,256]{1,0:T(8,128)(2,1)S(1)}, u32[]{:S(2)}, u32[]{:S(2)}) collective-permute-start(bf16[256,256]{1,0:T(8,128)(2,1)S(1)} %bitcast.151), channel_id=1, source_target_pairs={{32,0},{64,32},{96,64},{128,96},{160,128},{192,160},{224,192},{33,... | collective-permute-start | bytes 393224 | tf_op jit(solution)/shard_map/ppermute | solution.py:13
  260.1 257.9 %all-reduce.3.cloned.1.call-start = ((), (), s32[]{:S(2)}) async-start(), calls=%async_computation.4 | async-start | bytes 1048576 | tf_op jit(solution)/shard_map/psum | solution.py:56
  366.9 9.3 %copy-start.2 = (bf16[256,256]{1,0:T(8,128)(2,1)S(1)}, bf16[256,256]{1,0:T(8,128)(2,1)}, u32[]{:S(2)}) copy-start(bf16[256,256]{1,0:T(8,128)(2,1)} %fusion.15) | copy-start | bytes 393220
  366.9 9.3 %copy-start.3 = (bf16[256,256]{1,0:T(8,128)(2,1)S(1)}, bf16[256,256]{1,0:T(8,128)(2,1)}, u32[]{:S(2)}) copy-start(bf16[256,256]{1,0:T(8,128)(2,1)} %fusion.16) | copy-start | bytes 393220
  366.9 9.3 %copy-start.4 = (bf16[256,256]{1,0:T(8,128)(2,1)S(1)}, bf16[256,256]{1,0:T(8,128)(2,1)}, u32[]{:S(2)}) copy-start(bf16[256,256]{1,0:T(8,128)(2,1)} %add_convert_fusion) | copy-start | bytes 393220
  374.9 226.4 %all-gather.11.cloned.1.call-start = ((), (), s32[]{:S(2)}) async-start(), calls=%async_computation.3 | async-start | bytes 4325376 | tf_op jit(solution)/shard_map/all_gather | solution.py:62
Sparse Core Ops, SparseCore 0:
  11.2 82.8 all-gather.4
  133.2 78.9 all-gather.6
  260.2 75.7 all-gather.8
  375.1 142.8 all-reduce.2
  520.7 80.5 all-gather.10
where the time goes:
time: 649 us; the launch traced here: 647 us
  waiting for transfers between devices  459 us (71%)
  local copies, waits for them, and re-layouts  86.5 us (13%)
  matrix products  75.5 us (12%)
  between operations  14.2 us (2%)
    all_gather x4, waiting for transfers between devices, shards(): gathered = lax.all_gather(image, 'rows', axis=0, tiled=True)  315 us
    psum x1, waiting for transfers between devices, shards(): weight_acc[layer] = weight_acc[layer] + lax.psum(term, 'rows')  140 us
    dot_general x4, local copies, waits for them, and re-layouts, tile_product(): jnp.einsum('kab,kbf->kaf', values, blocks, preferred_element_type=jnp.flo...  51 us
    dot_general x4, matrix products, tile_product(): jnp.einsum('kab,kbf->kaf', values, blocks, preferred_element_type=jnp.flo...  40.3 us
    gather x4, local copies, waits for them, and re-layouts, tile_product(): blocks = gathered.reshape(-1, tile, width)[index]  32.3 us
    dot_general x4, matrix products, tile_product(): jnp.einsum('ik,kaf->iaf', select, products, precision=lax.Precision.HIGHEST)  28.2 us
  transfers between devices with their start and end apart: 6, of which 6 were waited for; matrix products, arithmetic and copies ran while one was open for 2% of the time, Pallas kernels for 0%

commit v1 on v0

v1 whole, which is shorter than its diff:
```python
import jax
import jax.numpy as jnp
from jax import lax
from jax.experimental import pallas as pl
from jax.experimental.pallas import tpu as pltpu
from jax.sharding import PartitionSpec as P

ALPHA = 0.1
BETA_SCALE = 0.5
MESH = pl.DeviceIdType.MESH

SECTIONS = 8
XS = 4
ZS = 8
TILE = 128
WIDTH = 256
ROWS = 256
LIST = 96
CHUNKS = 24
F32 = jnp.float32
BF16 = jnp.bfloat16
I32 = jnp.int32


def kernel(
    grad_in, grad_last, support, preact, weights, vals_hbm, row_in, col_in, count_in,
    hand_out, init_out, wg_out,
    wg_acc, x_part, x_in, z_own, z_part, z_in, z_done, x_done,
    vals, key_buf, tab_v, tab_s, need, need_m, need_p, run, dense,
    full, half, pick, grad_buf, masked_buf, acc, handed,
    vals_sem, tab_sem, need_send, need_recv, full_send, full_recv, half_send, half_recv,
    hand_send, hand_recv, sum_xs, sum_xr, sum_zs, sum_zr, fin_zs, fin_zr, fin_xs, fin_xr,
):
    section = lax.axis_index("section")
    me = lax.axis_index("rows")
    x = me // ZS
    z = me % ZS

    def at(sec, xx, zz):
        return (sec, xx * ZS + zz)

    x_up = at(section, (x + 1) % XS, z)
    x_dn = at(section, (x + XS - 1) % XS, z)
    z_up = at(section, x, (z + 1) % ZS)
    z_dn = at(section, x, (z + ZS - 1) % ZS)
    s_up = at((section + 1) % SECTIONS, x, z)
    s_dn = at((section + SECTIONS - 1) % SECTIONS, x, z)

    for t in range(2):
        pltpu.make_async_copy(vals_hbm.at[0, t], vals.at[t], vals_sem.at[t]).start()

    barrier = pltpu.get_barrier_semaphore()
    across_x = [at(section, (x + d) % XS, z) for d in range(1, XS)]
    across_z = [at(section, x, (z + d) % ZS) for d in range(1, ZS)]
    peers = across_x + across_z + [s_up, s_dn]
    for peer in peers:
        pl.semaphore_signal(barrier, inc=1, device_id=peer, device_id_type=MESH)

    def remote(src, dst, send, recv, device):
        return pltpu.make_async_remote_copy(
            src_ref=src, dst_ref=dst, send_sem=send, recv_sem=recv,
            device_id=device, device_id_type=MESH,
        )

    def tile(h):
        return pl.ds(h * TILE, TILE)

    def send_up(i, c, k, h):
        k_to = (k + 7) % ZS
        return remote(
            full.at[i, c, k, tile(h)], full.at[i, c, k_to, tile(h)],
            full_send.at[0, c, k, h], full_recv.at[i, c, k_to, h], z_up,
        )

    def send_dn(i, c, k, h):
        k_to = (k + 1) % ZS
        return remote(
            full.at[i, c, k, tile(h)], full.at[i, c, k_to, tile(h)],
            full_send.at[1, c, k, h], full_recv.at[i, c, k_to, h], z_dn,
        )

    def send_side(i, h):
        return remote(
            full.at[i, 0, 0, tile(h)], full.at[i, 1, 0, tile(h)],
            full_send.at[2, 0, 0, h], full_recv.at[i, 1, 0, h], x_up,
        )

    def send_pick(i, c, k):
        return remote(
            pick.at[c, k], half.at[i, k, tile(c)],
            half_send.at[c, k], half_recv.at[i, c, k], x_dn if c == 0 else x_up,
        )

    def got_full(i, c, k, h):
        remote(
            full.at[i, c, k, tile(h)], full.at[i, c, k, tile(h)],
            full_send.at[0, c, k, h], full_recv.at[i, c, k, h], z_up,
        ).wait_recv()

    def got_half(i, c, k):
        remote(
            pick.at[c, k], half.at[i, k, tile(c)],
            half_send.at[c, k], half_recv.at[i, c, k], x_up,
        ).wait_recv()

    need_copies = [
        remote(need, need_m, need_send.at[0], need_recv.at[0], x_up),
        remote(need, need_p, need_send.at[1], need_recv.at[1], x_dn),
    ]

    def all_sends(i):
        copies = []
        for c in range(2):
            for k in (0, 7, 6):
                copies += [send_up(i, c, k, 0), send_up(i, c, k, 1)]
            copies.append(send_up(i, c, 5, 0))
            for k in (0, 1, 2):
                copies += [send_dn(i, c, k, 0), send_dn(i, c, k, 1)]
            copies.append(send_dn(i, c, 3, 1))
        copies += [send_side(i, 0), send_side(i, 1)]
        for c in range(2):
            for k in range(ZS):
                copies.append(send_pick(i, c, k))
        return copies

    def beta_of(layer):
        depth = (2 * section + layer + 1).astype(F32)
        return jnp.log(BETA_SCALE / jnp.full((8, 128), depth, F32) + 1.0)[0:1, 0:1]

    def find_needs():
        slot = lax.broadcasted_iota(I32, (16, LIST), 0)
        far = jnp.where(slot < 8, (x + 1) % XS, (x + 2) % XS)
        owner = far * ZS + (z + slot) % ZS
        for t in range(2):
            col = jnp.broadcast_to(col_in[0, t : t + 1, :], (16, LIST))
            second = jnp.where((col >> 1) == owner, (col & 1).astype(F32), 0.0)
            need[t * 16 : (t + 1) * 16, :] = jnp.broadcast_to(
                jnp.max(second, axis=1, keepdims=True), (16, 128)
            )

    def sort_entries(t):
        col = col_in[0, pl.ds(t, 1), :]
        owner = col >> 1
        dx = ((owner >> 3) - x) & 3
        dz = ((owner & 7) - z) & 7
        near = (dx == 0) | (dx == 3)
        chunk = jnp.where(near, jnp.where(dx == 3, 8 + dz, dz), 16 + dz)
        side = jnp.where(near, col & 1, dx - 1)
        key = chunk * 4 + side * 2 + row_in[0, pl.ds(t, 1), :]
        place = lax.broadcasted_iota(I32, (1, LIST), 1)
        key = jnp.where(place < count_in[0, pl.ds(t, 1), :], key, 127)
        key_buf[...] = jnp.full((8, 128), 127, I32)
        key_buf[0:1, 0:LIST] = key
        across = jnp.broadcast_to(key_buf[0:1, :], (128, 128))
        down = across.T
        lane = lax.broadcasted_iota(I32, (128, 128), 1)
        sub = lax.broadcasted_iota(I32, (128, 128), 0)

        def count(hit, axis):
            return jnp.sum(jnp.where(hit, 1, 0), axis=axis, keepdims=True)

        rank = count((across < down) | ((across == down) & (lane < sub)), 1)

        def pull(values, position):
            return jnp.sum(jnp.where(rank == position, values, 0), axis=0, keepdims=True)

        order = pull(sub, lane)
        same = jnp.where(
            (pull(down, lane) == pull(down, lane - 1)) & (lane[0:1, :] > 0), 1, 0
        )
        last = jnp.maximum(count(down <= lane, 0) - 1, 0)
        there = jnp.where(count(down == lane, 0) > 0, 1, 0)
        for r, line in enumerate((order, same, last, there)):
            tab_v[r : r + 1, :] = line
        fetch = pltpu.make_async_copy(tab_v, tab_s, tab_sem)
        fetch.start()
        fetch.wait()

    def build_dense(t):
        sort_entries(t)

        @pl.when(t == 0)
        def _():
            for u in range(2):
                pltpu.make_async_copy(vals_hbm.at[0, u], vals.at[u], vals_sem.at[u]).wait()

        def add(e, total):
            total = total * tab_s[1, e].astype(F32) + vals[t, tab_s[0, e]].astype(F32)
            run[e] = total
            return total

        lax.fori_loop(0, LIST, add, jnp.zeros((TILE, TILE), F32), unroll=4)

        def fill(j, carry):
            for side in range(2):
                for r in range(2):
                    slot = j * 4 + side * 2 + r
                    value = run[tab_s[2, slot]] * tab_s[3, slot].astype(F32)
                    dense[t, j, tile(r), tile(side)] = value.astype(BF16)
            return carry

        lax.fori_loop(0, CHUNKS, fill, 0)

    def sum_x(w, d):
        return remote(
            x_part.at[w, (x + d) % XS], x_in.at[w, d - 1],
            sum_xs.at[w, d - 1], sum_xr.at[w, d - 1], across_x[d - 1],
        )

    def sum_z(w, d):
        return remote(
            z_part.at[w, (z + d) % ZS], z_in.at[w, d - 1],
            sum_zs.at[w, d - 1], sum_zr.at[w, d - 1], across_z[d - 1],
        )

    def fin_z(w, d):
        return remote(
            z_done.at[w, z], z_done.at[w, z],
            fin_zs.at[w, d - 1], fin_zr.at[w, d - 1], across_z[d - 1],
        )

    def fin_x(w, d):
        return remote(
            x_done.at[w, x], x_done.at[w, x],
            fin_xs.at[w, d - 1], fin_xr.at[w, d - 1], across_x[d - 1],
        )

    def got_fin(ref, w, d, place, recv, device):
        remote(ref.at[w, place], ref.at[w, place], recv.at[w, d - 1], recv.at[w, d - 1], device).wait_recv()

    def scatter_x(w, total):
        x_part[w] = total.astype(BF16).reshape(XS, ROWS // XS, WIDTH)
        wg_acc[w] = total
        for d in range(1, XS):
            sum_x(w, d).start()

    def scatter_z(w):
        for d in range(1, XS):
            sum_x(w, d).wait_recv()
        total = wg_acc[w, pl.ds(x * (ROWS // XS), ROWS // XS)]
        for d in range(1, XS):
            total = total + x_in[w, d - 1].astype(F32)
        for q in range(ZS):
            part = total[16 * (q // 2) : 16 * (q // 2) + 16, 128 * (q % 2) : 128 * (q % 2) + 128]
            z_own[q] = part
            z_part[w, q] = part.astype(BF16)
        for d in range(1, ZS):
            sum_z(w, d).start()

    def gather_z(w):
        for d in range(1, ZS):
            sum_z(w, d).wait_recv()
        total = z_own[z]
        for d in range(1, ZS):
            total = total + z_in[w, d - 1].astype(F32)
        z_done[w, z] = total.astype(BF16)
        for d in range(1, ZS):
            fin_z(w, d).start()

    def gather_x(w):
        for d in range(1, ZS):
            got_fin(z_done, w, d, (z + ZS - d) % ZS, fin_zr, z_up)
        for q in range(ZS):
            x_done[w, x, 16 * (q // 2) : 16 * (q // 2) + 16, 128 * (q % 2) : 128 * (q % 2) + 128] = z_done[w, q]
        for d in range(1, XS):
            fin_x(w, d).start()

    def finish_sum(w):
        for d in range(1, XS):
            got_fin(x_done, w, d, (x + XS - d) % XS, fin_xr, x_up)
        for q in range(XS):
            wg_out[0, w, q * (ROWS // XS) : (q + 1) * (ROWS // XS)] = x_done[w, q].astype(F32)
        for d in range(1, XS):
            sum_x(w, d).wait_send()
            fin_x(w, d).wait_send()
        for d in range(1, ZS):
            sum_z(w, d).wait_send()
            fin_z(w, d).wait_send()

    def step(i, carry):
        t = i // 2
        layer = 1 - i % 2
        beta = beta_of(layer)

        @pl.when(i == 0)
        def _():
            grad_buf[...] = grad_in[0]

        @pl.when(i == 2)
        def _():
            remote(grad_buf, handed, hand_send, hand_recv, s_dn).wait()
            last = jnp.full((8, 128), section, I32)[0:1, 0:1] == SECTIONS - 1
            grad_buf[...] = jnp.where(
                last, grad_last[...].astype(F32), handed[...].astype(F32)
            ).astype(BF16)

        live = preact[0, t, layer].astype(F32) > 0
        masked32 = jnp.where(live, grad_buf[...].astype(F32), 0.0)
        masked = masked32.astype(BF16)
        masked_buf[...] = masked
        turned = lax.dot_general(
            masked, weights[0, layer], (((1,), (1,)), ((), ())), preferred_element_type=F32
        )
        image = ((1.0 - beta) * masked32 + beta * turned).astype(BF16)
        full[i, 0, 0] = image

        @pl.when(i == 0)
        def _():
            pl.semaphore_wait(barrier, len(peers))

        for h in range(2):
            send_side(i, h).start()
            send_up(i, 0, 0, h).start()
            send_dn(i, 0, 0, h).start()

        @pl.when(i == 0)
        def _():
            find_needs()
            for copy in need_copies:
                copy.start()

        @pl.when(i < 2)
        def _():
            build_dense(i)

        @pl.when(i == 0)
        def _():
            for copy in need_copies:
                copy.wait()

        def relay(c, m, h):
            up, dn = 8 - m, m
            if m < 4 or h == 0:
                got_full(i, c, up, h)
                if m < 3 or (m == 3 and h == 0):
                    send_up(i, c, up, h).start()
            if m < 4 or h == 1:
                got_full(i, c, dn, h)
                if m < 3 or (m == 3 and h == 1):
                    send_dn(i, c, dn, h).start()

        def pass_on(c, k):
            table = need_m if c == 0 else need_p
            line = table[pl.ds(t * 16 + c * 8 + k, 1), :].astype(BF16)
            second = jnp.concatenate([line, line], axis=1)
            first = 1.0 - second
            pick[c, k] = full[i, c, k, tile(0)] * first + full[i, c, k, tile(1)] * second
            send_pick(i, c, k).start()

        def product(j):
            block = full[i, j // 8, j % 8] if j < 16 else half[i, j - 16]
            return jnp.dot(dense[t, j], block, preferred_element_type=F32)

        def add_products(chunks):
            acc[...] += sum(product(j) for j in chunks)

        for h in range(2):
            got_full(i, 1, 0, h)
            send_up(i, 1, 0, h).start()
            send_dn(i, 1, 0, h).start()
        pass_on(0, 0)
        pass_on(1, 0)
        shown = ALPHA * full[i, 0, 0].astype(F32)
        term = beta * lax.dot_general(
            support[0, t, layer], masked_buf[...], (((0,), (0,)), ((), ())),
            preferred_element_type=F32,
        )

        @pl.when(layer == 1)
        def _():
            init_out[0, t] = shown

        @pl.when(layer == 0)
        def _():
            init_out[0, t] += shown

        @pl.when(t == 0)
        def _():
            wg_acc[layer] = term

        @pl.when(t == 1)
        def _():
            scatter_x(layer, wg_acc[layer] + term)

        acc[...] = product(0) + product(8)

        for m in range(1, 5):
            ks = (8 - m, m) if m < 4 else (4,)
            for c in range(2):
                for h in range(2):
                    relay(c, m, h)
                for k in ks:
                    pass_on(c, k)
                add_products([8 * c + k for k in ks])
            before = (9 - m, m - 1) if m > 1 else (0,)
            for k in before:
                got_half(i, 0, k)
                got_half(i, 1, k)
            add_products([16 + k for k in before])

            @pl.when(t == 1)
            def _():
                if m == 1:
                    scatter_z(layer)
                elif m == 2:
                    gather_z(layer)
                elif m == 3:
                    gather_x(layer)

        for c in range(2):
            got_half(i, c, 4)
        grad = ((1.0 - ALPHA) * (acc[...] + product(20))).astype(BF16)
        grad_buf[...] = grad

        @pl.when(layer == 0)
        def _():
            hand_out[t, 0] = grad

        @pl.when(i == 1)
        def _():
            remote(grad_buf, handed, hand_send, hand_recv, s_dn).start()

        @pl.when(t == 1)
        def _():
            finish_sum(layer)

        for copy in all_sends(i):
            copy.wait_send()
        return carry

    lax.fori_loop(0, 4, step, 0)


def write_results(*refs):
    sources, targets, staged, (in_sem, out_sem) = refs[:3], refs[3:6], refs[6:9], refs[9:]
    come = [pltpu.make_async_copy(a, b, in_sem.at[n]) for n, (a, b) in enumerate(zip(sources, staged))]
    go = [pltpu.make_async_copy(a, b, out_sem.at[n]) for n, (a, b) in enumerate(zip(staged, targets))]
    for copy in come:
        copy.start()
    for first, second in zip(come, go):
        first.wait()
        second.start()
    for copy in go:
        copy.wait()


def shards(grad_in, grad_last, support, preact, weights, tile_vals, tile_row, tile_col, tile_count):
    vmem = pl.BlockSpec(memory_space=pltpu.VMEM)
    shapes = (
        jax.ShapeDtypeStruct((2, 1, ROWS, WIDTH), BF16),
        jax.ShapeDtypeStruct((1, 2, ROWS, WIDTH), F32),
        jax.ShapeDtypeStruct((1, 2, WIDTH, WIDTH), F32),
    )
    results = pl.pallas_call(
        kernel,
        out_shape=shapes,
        in_specs=[vmem] * 5
        + [pl.BlockSpec(memory_space=pl.ANY), vmem, vmem, vmem],
        out_specs=(vmem, vmem, vmem),
        scratch_shapes=[
            pltpu.VMEM((2, WIDTH, WIDTH), F32),
            pltpu.VMEM((2, XS, ROWS // XS, WIDTH), BF16),
            pltpu.VMEM((2, XS - 1, ROWS // XS, WIDTH), BF16),
            pltpu.VMEM((ZS, 16, 128), F32),
            pltpu.VMEM((2, ZS, 16, 128), BF16),
            pltpu.VMEM((2, ZS - 1, 16, 128), BF16),
            pltpu.VMEM((2, ZS, 16, 128), BF16),
            pltpu.VMEM((2, XS, ROWS // XS, WIDTH), BF16),
            pltpu.VMEM((2, LIST, TILE, TILE), BF16),
            pltpu.VMEM((8, 128), I32),
            pltpu.VMEM((8, 128), I32),
            pltpu.SMEM((8, 128), I32),
            pltpu.VMEM((32, 128), F32),
            pltpu.VMEM((32, 128), F32),
            pltpu.VMEM((32, 128), F32),
            pltpu.VMEM((LIST, TILE, TILE), F32),
            pltpu.VMEM((2, CHUNKS, 256, 256), BF16),
            pltpu.VMEM((4, 2, ZS, ROWS, WIDTH), BF16),
            pltpu.VMEM((4, ZS, 2 * TILE, WIDTH), BF16),
            pltpu.VMEM((2, ZS, TILE, WIDTH), BF16),
            pltpu.VMEM((ROWS, WIDTH), BF16),
            pltpu.VMEM((ROWS, WIDTH), BF16),
            pltpu.VMEM((ROWS, WIDTH), F32),
            pltpu.VMEM((ROWS, WIDTH), BF16),
            pltpu.SemaphoreType.DMA((2,)),
            pltpu.SemaphoreType.DMA,
            pltpu.SemaphoreType.DMA((2,)),
            pltpu.SemaphoreType.DMA((2,)),
            pltpu.SemaphoreType.DMA((3, 2, ZS, 2)),
            pltpu.SemaphoreType.DMA((4, 2, ZS, 2)),
            pltpu.SemaphoreType.DMA((2, ZS)),
            pltpu.SemaphoreType.DMA((4, 2, ZS)),
            pltpu.SemaphoreType.DMA,
            pltpu.SemaphoreType.DMA,
        ]
        + [pltpu.SemaphoreType.DMA((2, n - 1)) for n in (XS, XS, ZS, ZS, ZS, ZS, XS, XS)],
        compiler_params=pltpu.CompilerParams(
            collective_id=0, has_side_effects=True, vmem_limit_bytes=60 * 1024 * 1024
        ),
    )(grad_in, grad_last, support, preact, weights, tile_vals, tile_row, tile_col, tile_count)
    anywhere = pl.BlockSpec(memory_space=pl.ANY)
    return pl.pallas_call(
        write_results,
        out_shape=shapes,
        in_specs=[anywhere] * 3,
        out_specs=(anywhere,) * 3,
        scratch_shapes=[pltpu.VMEM(s.shape, s.dtype) for s in shapes]
        + [pltpu.SemaphoreType.DMA((3,)), pltpu.SemaphoreType.DMA((3,))],
    )(*results)


def solution(mesh):
    return jax.shard_map(
        shards,
        mesh=mesh,
        in_specs=(
            P("section", "rows", None),
            P("rows", None),
            P("section", None, None, "rows", None),
            P("section", None, None, "rows", None),
            P("section", None, None, None),
            P("section", None, "rows", None, None),
            P("section", None, "rows"),
            P("section", None, "rows"),
            P("section", None, "rows"),
        ),
        out_specs=(
            P(None, "section", "rows", None),
            P("section", None, "rows", None),
            P("section", None, None, None),
        ),
        check_vma=False,
    )
```

time: 649 us -> 136 us (0.21)
  waiting for transfers between devices: 459 us -> 0 us
  Pallas kernels: 0 us -> 132 us
  local copies, waits for them, and re-layouts: 86.5 us -> 1.3 us
  matrix products: 75.5 us -> 0 us
  between operations: 14.2 us -> 0.64 us
    all_gather x4 -> x0, waiting for transfers between devices: 315 us -> none  [shards(): gathered = lax.all_gather(image, 'rows', axis=0, tiled=True)]
    psum x1 -> x0, waiting for transfers between devices: 140 us -> none  [shards(): weight_acc[layer] = weight_acc[layer] + lax.psum(term, 'rows')]
    pallas_call x0 -> x2, Pallas kernels: none -> 132 us  [the longest x1 130 us: shards(): pl.pallas_call(kernel, out_shape=shapes, in_specs=[vmem] * 5 + [pl.BlockS...]
    dot_general x16 -> x0, matrix products: 75.5 us -> none  [the longest x4 40.3 us: tile_product(): jnp.einsum('kab,kbf->kaf', values, blocks, preferred_element_type=jnp.flo...]
    dot_general x4 -> x0, local copies, waits for them, and re-layouts: 51 us -> none  [tile_product(): jnp.einsum('kab,kbf->kaf', values, blocks, preferred_element_type=jnp.flo...]
    gather x4 -> x0, local copies, waits for them, and re-layouts: 32.3 us -> none  [tile_product(): blocks = gathered.reshape(-1, tile, width)[index]]
  transfers between devices with their start and end apart: 6 -> 0, of which waited for: 6 -> 0; matrix products, arithmetic and copies ran while one was open for 2% -> 0% of each run, Pallas kernels for 0% -> 0%
where the time goes in v1:
time: 136 us; the launch traced here: 134 us
  Pallas kernels  132 us (97%)
    pallas_call x1, Pallas kernels, shards(): pl.pallas_call(kernel, out_shape=shapes, in_specs=[vmem] * 5 + [pl.BlockS...  130 us

profile of v1, /device:TPU:1, one launch (start us, length us, event | category | flops | bytes accessed | tf_op | source)
XLA Modules:
  0.0 134.4 jit_solution(10638336250439939215)
XLA Ops:
  0.6 1.3 copy.12.count_in
  1.9 130.3 %shard_map.112 = (bf16[2,1,256,256]{3,2,1,0:T(8,128)(2,1)}, f32[1,2,256,256]{3,2,1,0:T(8,128)}, f32[1,2,256,256]{3,2,1,0:T(8,128)}) custom-call(bf16[1,256,256]{2,1,0:T(8,128)(2,1)} %grad_in.1, bf16[256,256]{1,0:T(8,128)(2,1)} %grad_last.1, bf16[1,2,2,256,256]{4,3,2,1,0:T(8,128)(2,1)} %support.1, bf16[1,2,2,256,256]{4,3,2,1,0:T(8,128)(2,1)} %preact.1, ...), custom_call_target="tpu_custom_call" | custom-call | tf_op jit(solution)/shard_map/pallas_call | solution.py:454
  132.2 2.1 %shard_map.113 = (bf16[2,1,256,256]{3,2,1,0:T(8,128)(2,1)}, f32[1,2,256,256]{3,2,1,0:T(8,128)}, f32[1,2,256,256]{3,2,1,0:T(8,128)}) custom-call(bf16[2,1,256,256]{3,2,1,0:T(8,128)(2,1)} %get-tuple-element.6.refs_0_, f32[1,2,256,256]{3,2,1,0:T(8,128)} %get-tuple-element.7.refs_1_, f32[1,2,256,256]{3,2,1,0:T(8,128)} %get-tuple-element.8.refs_2_), custom_call_target="tpu_custom_call" | custom-call | tf_op jit(solution)/shard_map/pallas_call | solution.py:502

commit v2 on v1

v2 whole, which is shorter than its diff:
```python
import jax
import jax.numpy as jnp
from jax import lax
from jax.experimental import pallas as pl
from jax.experimental.pallas import tpu as pltpu
from jax.sharding import PartitionSpec as P

ALPHA = 0.1
BETA_SCALE = 0.5
MESH = pl.DeviceIdType.MESH

SECTIONS = 8
XS = 4
ZS = 8
TILE = 128
WIDTH = 256
ROWS = 256
LIST = 96
RA = 64
RC = TILE - RA
ARRIVALS = (
    (1, 0, 0), (1, 0, 1), (0, 7, 0), (0, 1, 0), (0, 7, 1), (0, 1, 1), (1, 7, 0), (1, 1, 0), (1, 7, 1), (1, 1, 1),
    (0,),
    (0, 6, 0), (0, 2, 0), (0, 6, 1), (0, 2, 1), (1, 6, 0), (1, 2, 0), (1, 6, 1), (1, 2, 1),
    (7,), (0, 5, 0), (0, 3, 0), (1,),
    (0, 5, 1), (0, 3, 1), (1, 5, 0), (1, 3, 0), (1, 5, 1), (1, 3, 1),
    (6,), (0, 4, 0), (2,), (1, 4, 0), (0, 4, 1), (1, 4, 1), (5,), (3,), (4,),
)
F32 = jnp.float32
BF16 = jnp.bfloat16
I32 = jnp.int32


def kernel(
    grad_in, grad_last, support, preact, weights, vals_hbm, row_in, col_in, count_in,
    hand_out, init_out, wg_out,
    wg_acc, x_part, x_in, z_own, z_part, z_in, z_done, x_done,
    vals, key_buf, tab_v, tab_s, need, need_at, run, near_adj, far_adj,
    full, side, far, pick1, pick2a, pick3, pick2c, grad_buf, masked_buf, acc, handed,
    vals_sem, tab_sem, need_send, need_recv, full_up, full_dn, full_recv,
    side_first, side_up, side_dn, side_recv, far_send, far_recv,
    hand_send, hand_recv, sum_xs, sum_xr, sum_zs, sum_zr, fin_zs, fin_zr, fin_xs, fin_xr,
):
    section = lax.axis_index("section")
    me = lax.axis_index("rows")
    x = me // ZS
    z = me % ZS

    def at(sec, xx, zz):
        return (sec, xx * ZS + zz)

    across_x = [at(section, (x + d) % XS, z) for d in range(1, XS)]
    across_z = [at(section, x, (z + d) % ZS) for d in range(1, ZS)]
    x_up, x_far, x_dn = across_x
    z_up, z_dn = across_z[0], across_z[-1]
    s_up = at((section + 1) % SECTIONS, x, z)
    s_dn = at((section + SECTIONS - 1) % SECTIONS, x, z)

    for t in range(2):
        pltpu.make_async_copy(vals_hbm.at[0, t], vals.at[t], vals_sem.at[t]).start()

    barrier = pltpu.get_barrier_semaphore()
    peers = across_x + across_z + [s_up, s_dn]
    for peer in peers:
        pl.semaphore_signal(barrier, inc=1, device_id=peer, device_id_type=MESH)

    def remote(src, dst, send, recv, device):
        return pltpu.make_async_remote_copy(
            src_ref=src, dst_ref=dst, send_sem=send, recv_sem=recv,
            device_id=device, device_id_type=MESH,
        )

    def tile(h):
        return pl.ds(h * TILE, TILE)

    def late(h):
        return pl.ds(h * RC, RC)

    def send_full(i, k, h, up):
        k_to = (k + (7 if up else 1)) % ZS
        return remote(
            full.at[i, k, tile(h)], full.at[i, k_to, tile(h)],
            (full_up if up else full_dn).at[k, h], full_recv.at[i, k_to, h], z_up if up else z_dn,
        )

    def send_side(i, k, h, up):
        k_to = (k + (7 if up else 1)) % ZS
        return remote(
            side.at[i, k, late(h)], side.at[i, k_to, late(h)],
            (side_up if up else side_dn).at[k, h], side_recv.at[i, k_to, h], z_up if up else z_dn,
        )

    def first_side(i, h):
        return remote(
            full.at[i, 0, pl.ds(h * TILE + RA, RC)], side.at[i, 0, late(h)],
            side_first.at[h], side_recv.at[i, 0, h], x_up,
        )

    def send_far(i, k, n):
        source, start, size, device = (
            (pick1.at[k], 0, TILE, x_dn),
            (pick2a.at[k], TILE, RA, x_far),
            (pick3.at[k], 2 * TILE, RA, x_up),
            (pick2c.at[k], TILE + RA, RC, x_up),
        )[n]
        return remote(
            source, far.at[i, k, pl.ds(start, size)], far_send.at[n, k], far_recv.at[i, n, k], device
        )

    def moves(c, k, h):
        up = k in (0, 7, 6) or (k == 5 and h == 0)
        dn = k in (0, 1, 2) or (k == 3 and h == 1)
        return [way for way, goes in ((True, up), (False, dn)) if goes]

    need_copies = [
        remote(need, need_at.at[n], need_send.at[n], need_recv.at[n], device)
        for n, device in enumerate((x_up, x_far, x_dn))
    ]

    def all_sends(i):
        copies = [first_side(i, h) for h in range(2)]
        for k in range(ZS):
            for h in range(2):
                for way in moves(0, k, h):
                    copies += [send_full(i, k, h, way), send_side(i, k, h, way)]
            copies += [send_far(i, k, n) for n in range(4)]
        return copies

    def beta_of(layer):
        depth = (2 * section + layer + 1).astype(F32)
        return jnp.log(BETA_SCALE / jnp.full((8, 128), depth, F32) + 1.0)[0:1, 0:1]

    def find_needs():
        slot = lax.broadcasted_iota(I32, (24, LIST), 0)
        owner = ((x + 1 + (slot >> 3)) & 3) * ZS + ((z + slot) & 7)
        for t in range(2):
            col = jnp.broadcast_to(col_in[0, t : t + 1, :], (24, LIST))
            second = jnp.where((col >> 1) == owner, (col & 1).astype(F32), 0.0)
            need[t * 24 : (t + 1) * 24, :] = jnp.broadcast_to(
                jnp.max(second, axis=1, keepdims=True), (24, 128)
            )

    def sort_entries(t):
        col = col_in[0, t : t + 1, :]
        owner = col >> 1
        dx = ((owner >> 3) - x) & 3
        dz = ((owner & 7) - z) & 7
        key = jnp.where(dx == 0, dz * 4 + (col & 1) * 2, 32 + dz * 6 + (dx - 1) * 2)
        key = key + row_in[0, t : t + 1, :]
        place = lax.broadcasted_iota(I32, (1, LIST), 1)
        key = jnp.where(place < count_in[0, :, t : t + 1], key, 127)
        key_buf[...] = jnp.full((8, 128), 127, I32)
        key_buf[0:1, 0:LIST] = key
        across = jnp.broadcast_to(key_buf[0:1, :], (128, 128))
        down = across.T
        lane = lax.broadcasted_iota(I32, (128, 128), 1)
        sub = lax.broadcasted_iota(I32, (128, 128), 0)

        def count(hit, axis):
            return jnp.sum(jnp.where(hit, 1, 0), axis=axis, keepdims=True)

        rank = count((across < down) | ((across == down) & (lane < sub)), 1)

        def pull(values, position):
            return jnp.sum(jnp.where(rank == position, values, 0), axis=0, keepdims=True)

        order = pull(sub, lane)
        same = jnp.where(
            (pull(down, lane) == pull(down, lane - 1)) & (lane[0:1, :] > 0), 1, 0
        )
        last = jnp.maximum(count(down <= lane, 0) - 1, 0)
        there = jnp.where(count(down == lane, 0) > 0, 1, 0)
        for r, line in enumerate((order, same, last, there)):
            tab_v[r : r + 1, :] = line
        fetch = pltpu.make_async_copy(tab_v, tab_s, tab_sem)
        fetch.start()
        fetch.wait()

    def build_adjacency(t):
        sort_entries(t)

        def add(e, total):
            total = total * tab_s[1, e].astype(F32) + vals[t, tab_s[0, e]].astype(F32)
            run[e] = total
            return total

        lax.fori_loop(0, LIST, add, jnp.zeros((TILE, TILE), F32), unroll=4)

        def summed(slot):
            return (run[tab_s[2, slot]] * tab_s[3, slot].astype(F32)).astype(BF16)

        def fill(k, carry):
            for r in range(2):
                for h in range(2):
                    near_adj[t, k, tile(r), tile(h)] = summed(k * 4 + h * 2 + r)
                for q in range(3):
                    far_adj[t, k, tile(r), tile(q)] = summed(32 + k * 6 + q * 2 + r)
            return carry

        lax.fori_loop(0, ZS, fill, 0)

    def sum_x(w, d):
        return remote(
            x_part.at[w, (x + d) % XS], x_in.at[w, d - 1],
            sum_xs.at[w, d - 1], sum_xr.at[w, d - 1], across_x[d - 1],
        )

    def sum_z(w, d):
        return remote(
            z_part.at[w, (z + d) % ZS], z_in.at[w, d - 1],
            sum_zs.at[w, d - 1], sum_zr.at[w, d - 1], across_z[d - 1],
        )

    def fin_z(w, d):
        return remote(
            z_done.at[w, z], z_done.at[w, z],
            fin_zs.at[w, d - 1], fin_zr.at[w, d - 1], across_z[d - 1],
        )

    def fin_x(w, d):
        return remote(
            x_done.at[w, x], x_done.at[w, x],
            fin_xs.at[w, d - 1], fin_xr.at[w, d - 1], across_x[d - 1],
        )

    def got_fin(ref, w, d, place, recv, device):
        remote(ref.at[w, place], ref.at[w, place], recv.at[w, d - 1], recv.at[w, d - 1], device).wait_recv()

    def scatter_x(w, total):
        x_part[w] = total.astype(BF16).reshape(XS, ROWS // XS, WIDTH)
        wg_acc[w] = total
        for d in range(1, XS):
            sum_x(w, d).start()

    def scatter_z(w):
        for d in range(1, XS):
            sum_x(w, d).wait_recv()
        total = wg_acc[w, pl.ds(x * (ROWS // XS), ROWS // XS)]
        for d in range(1, XS):
            total = total + x_in[w, d - 1].astype(F32)
        for q in range(ZS):
            part = total[16 * (q // 2) : 16 * (q // 2) + 16, 128 * (q % 2) : 128 * (q % 2) + 128]
            z_own[q] = part
            z_part[w, q] = part.astype(BF16)
        for d in range(1, ZS):
            sum_z(w, d).start()

    def gather_z(w):
        for d in range(1, ZS):
            sum_z(w, d).wait_recv()
        total = z_own[z]
        for d in range(1, ZS):
            total = total + z_in[w, d - 1].astype(F32)
        z_done[w, z] = total.astype(BF16)
        for d in range(1, ZS):
            fin_z(w, d).start()

    def gather_x(w):
        for d in range(1, ZS):
            got_fin(z_done, w, d, (z + ZS - d) % ZS, fin_zr, z_up)
        for q in range(ZS):
            x_done[w, x, 16 * (q // 2) : 16 * (q // 2) + 16, 128 * (q % 2) : 128 * (q % 2) + 128] = z_done[w, q]
        for d in range(1, XS):
            fin_x(w, d).start()

    def finish_sum(w):
        for d in range(1, XS):
            got_fin(x_done, w, d, (x + XS - d) % XS, fin_xr, x_up)
        for q in range(XS):
            wg_out[0, w, q * (ROWS // XS) : (q + 1) * (ROWS // XS)] = x_done[w, q].astype(F32)
        for d in range(1, XS):
            sum_x(w, d).wait_send()
            fin_x(w, d).wait_send()
        for d in range(1, ZS):
            sum_z(w, d).wait_send()
            fin_z(w, d).wait_send()

    find_needs()

    def step(i, carry):
        t = i // 2
        layer = 1 - i % 2
        beta = beta_of(layer)

        @pl.when(i == 0)
        def _():
            grad_buf[...] = grad_in[0]
            pl.semaphore_wait(barrier, len(peers))
            for copy in need_copies:
                copy.start()

        @pl.when(i == 2)
        def _():
            remote(grad_buf, handed, hand_send, hand_recv, s_dn).wait()
            last = jnp.full((8, 128), section, I32)[0:1, 0:1] == SECTIONS - 1
            grad_buf[...] = jnp.where(
                last, grad_last[...].astype(F32), handed[...].astype(F32)
            ).astype(BF16)

        for h in range(2):
            live = preact[0, t, layer, tile(h)].astype(F32) > 0
            masked32 = jnp.where(live, grad_buf[tile(h)].astype(F32), 0.0)
            masked = masked32.astype(BF16)
            masked_buf[tile(h)] = masked
            turned = lax.dot_general(
                masked, weights[0, layer], (((1,), (1,)), ((), ())), preferred_element_type=F32
            )
            full[i, 0, tile(h)] = ((1.0 - beta) * masked32 + beta * turned).astype(BF16)
            first_side(i, h).start()
            for way in (True, False):
                send_full(i, 0, h, way).start()

        shown = ALPHA * full[i, 0].astype(F32)
        term = beta * lax.dot_general(
            support[0, t, layer], masked_buf[...], (((0,), (0,)), ((), ())),
            preferred_element_type=F32,
        )

        @pl.when(t == 0)
        def _():
            wg_acc[layer] = term

        @pl.when(t == 1)
        def _():
            scatter_x(layer, wg_acc[layer] + term)

        @pl.when(layer == 1)
        def _():
            init_out[0, t] = shown

        @pl.when(layer == 0)
        def _():
            init_out[0, t] += shown

        @pl.when(i == 0)
        def _():
            for u in range(2):
                pltpu.make_async_copy(vals_hbm.at[0, u], vals.at[u], vals_sem.at[u]).wait()
            build_adjacency(0)
            for copy in need_copies:
                copy.wait()

        def chosen(table, q, k):
            line = table[pl.ds(t * 24 + (q - 1) * 8 + k, 1), :].astype(BF16)
            second = jnp.concatenate([line, line], axis=1)
            return 1.0 - second, second

        from_dn, from_far, from_up = (need_at.at[n] for n in range(3))

        def pass_full(k):
            for table, q, n, target, rows in (
                (from_dn, 1, 0, pick1, TILE), (from_far, 2, 1, pick2a, RA), (from_up, 3, 2, pick3, RA)
            ):
                first, second = chosen(table, q, k)
                target[k] = (
                    full[i, k, 0:rows] * first + full[i, k, TILE : TILE + rows] * second
                )
                send_far(i, k, n).start()

        def pass_side(k):
            first, second = chosen(from_up, 2, k)
            pick2c[k] = side[i, k, 0:RC] * first + side[i, k, RC : 2 * RC] * second
            send_far(i, k, 3).start()
            first, second = chosen(need, 3, k)
            far[i, k, 2 * TILE + RA : 3 * TILE] = (
                side[i, k, 0:RC] * first + side[i, k, RC : 2 * RC] * second
            )

        def product(k, near):
            adjacency, block = (near_adj[t, k], full[i, k]) if near else (far_adj[t, k], far[i, k])
            return jnp.dot(adjacency, block, preferred_element_type=F32)

        pass_full(0)

        @pl.when(i == 1)
        def _():
            build_adjacency(1)

        acc[...] = product(0, True)

        for n, arrival in enumerate(ARRIVALS):
            if len(arrival) == 1:
                (k,) = arrival
                for part in range(4):
                    send_far(i, k, part).wait_recv()
                if k != 4:
                    acc[...] += product(k, False)
            else:
                c, k, h = arrival
                if c == 0:
                    remote(
                        full.at[i, k, tile(h)], full.at[i, k, tile(h)],
                        full_up.at[k, h], full_recv.at[i, k, h], z_up,
                    ).wait_recv()
                else:
                    remote(
                        side.at[i, k, late(h)], side.at[i, k, late(h)],
                        side_up.at[k, h], side_recv.at[i, k, h], z_up,
                    ).wait_recv()
                for way in moves(c, k, h):
                    (send_side if c else send_full)(i, k, h, way).start()
                if h == 1:
                    if c:
                        pass_side(k)
                    else:
                        pass_full(k)
                        acc[...] += product(k, True)

            @pl.when(t == 1)
            def _():
                if arrival == (0,):
                    scatter_z(layer)
                elif arrival == (7,):
                    gather_z(layer)
                elif arrival == (6,):
                    gather_x(layer)

        grad = ((1.0 - ALPHA) * (acc[...] + product(4, False))).astype(BF16)
        grad_buf[...] = grad

        @pl.when(i == 1)
        def _():
            remote(grad_buf, handed, hand_send, hand_recv, s_dn).start()

        @pl.when(layer == 0)
        def _():
            hand_out[t, 0] = grad

        @pl.when(t == 1)
        def _():
            finish_sum(layer)

        for copy in all_sends(i):
            copy.wait_send()
        return carry

    lax.fori_loop(0, 4, step, 0)


def write_results(*refs):
    sources, targets, staged, (in_sem, out_sem) = refs[:3], refs[3:6], refs[6:9], refs[9:]
    come = [pltpu.make_async_copy(a, b, in_sem.at[n]) for n, (a, b) in enumerate(zip(sources, staged))]
    go = [pltpu.make_async_copy(a, b, out_sem.at[n]) for n, (a, b) in enumerate(zip(staged, targets))]
    for copy in come:
        copy.start()
    for first, second in zip(come, go):
        first.wait()
        second.start()
    for copy in go:
        copy.wait()


def shards(grad_in, grad_last, support, preact, weights, tile_vals, tile_row, tile_col, tile_count):
    vmem = pl.BlockSpec(memory_space=pltpu.VMEM)
    shapes = (
        jax.ShapeDtypeStruct((2, 1, ROWS, WIDTH), BF16),
        jax.ShapeDtypeStruct((1, 2, ROWS, WIDTH), F32),
        jax.ShapeDtypeStruct((1, 2, WIDTH, WIDTH), F32),
    )
    results = pl.pallas_call(
        kernel,
        out_shape=shapes,
        in_specs=[vmem] * 5
        + [pl.BlockSpec(memory_space=pl.ANY), vmem, vmem, vmem],
        out_specs=(vmem, vmem, vmem),
        scratch_shapes=[
            pltpu.VMEM((2, WIDTH, WIDTH), F32),
            pltpu.VMEM((2, XS, ROWS // XS, WIDTH), BF16),
            pltpu.VMEM((2, XS - 1, ROWS // XS, WIDTH), BF16),
            pltpu.VMEM((ZS, 16, 128), F32),
            pltpu.VMEM((2, ZS, 16, 128), BF16),
            pltpu.VMEM((2, ZS - 1, 16, 128), BF16),
            pltpu.VMEM((2, ZS, 16, 128), BF16),
            pltpu.VMEM((2, XS, ROWS // XS, WIDTH), BF16),
            pltpu.VMEM((2, LIST, TILE, TILE), BF16),
            pltpu.VMEM((8, 128), I32),
            pltpu.VMEM((8, 128), I32),
            pltpu.SMEM((8, 128), I32),
            pltpu.VMEM((48, 128), F32),
            pltpu.VMEM((3, 48, 128), F32),
            pltpu.VMEM((LIST, TILE, TILE), F32),
            pltpu.VMEM((2, ZS, ROWS, 2 * TILE), BF16),
            pltpu.VMEM((2, ZS, ROWS, 3 * TILE), BF16),
            pltpu.VMEM((4, ZS, ROWS, WIDTH), BF16),
            pltpu.VMEM((4, ZS, 2 * RC, WIDTH), BF16),
            pltpu.VMEM((4, ZS, 3 * TILE, WIDTH), BF16),
            pltpu.VMEM((ZS, TILE, WIDTH), BF16),
            pltpu.VMEM((ZS, RA, WIDTH), BF16),
            pltpu.VMEM((ZS, RA, WIDTH), BF16),
            pltpu.VMEM((ZS, RC, WIDTH), BF16),
            pltpu.VMEM((ROWS, WIDTH), BF16),
            pltpu.VMEM((ROWS, WIDTH), BF16),
            pltpu.VMEM((ROWS, WIDTH), F32),
            pltpu.VMEM((ROWS, WIDTH), BF16),
            pltpu.SemaphoreType.DMA((2,)),
            pltpu.SemaphoreType.DMA,
            pltpu.SemaphoreType.DMA((3,)),
            pltpu.SemaphoreType.DMA((3,)),
            pltpu.SemaphoreType.DMA((ZS, 2)),
            pltpu.SemaphoreType.DMA((ZS, 2)),
            pltpu.SemaphoreType.DMA((4, ZS, 2)),
            pltpu.SemaphoreType.DMA((2,)),
            pltpu.SemaphoreType.DMA((ZS, 2)),
            pltpu.SemaphoreType.DMA((ZS, 2)),
            pltpu.SemaphoreType.DMA((4, ZS, 2)),
            pltpu.SemaphoreType.DMA((4, ZS)),
            pltpu.SemaphoreType.DMA((4, 4, ZS)),
            pltpu.SemaphoreType.DMA,
            pltpu.SemaphoreType.DMA,
        ]
        + [pltpu.SemaphoreType.DMA((2, n - 1)) for n in (XS, XS, ZS, ZS, ZS, ZS, XS, XS)],
        compiler_params=pltpu.CompilerParams(
            collective_id=0, has_side_effects=True, vmem_limit_bytes=60 * 1024 * 1024
        ),
    )(grad_in, grad_last, support, preact, weights, tile_vals, tile_row, tile_col, jnp.swapaxes(tile_count, 1, 2))
    anywhere = pl.BlockSpec(memory_space=pl.ANY)
    return pl.pallas_call(
        write_results,
        out_shape=shapes,
        in_specs=[anywhere] * 3,
        out_specs=(anywhere,) * 3,
        scratch_shapes=[pltpu.VMEM(s.shape, s.dtype) for s in shapes]
        + [pltpu.SemaphoreType.DMA((3,)), pltpu.SemaphoreType.DMA((3,))],
    )(*results)


def solution(mesh):
    return jax.shard_map(
        shards,
        mesh=mesh,
        in_specs=(
            P("section", "rows", None),
            P("rows", None),
            P("section", None, None, "rows", None),
            P("section", None, None, "rows", None),
            P("section", None, None, None),
            P("section", None, "rows", None, None),
            P("section", None, "rows"),
            P("section", None, "rows"),
            P("section", None, "rows"),
        ),
        out_specs=(
            P(None, "section", "rows", None),
            P("section", None, "rows", None),
            P("section", None, None, None),
        ),
        check_vma=False,
    )
```

time: 136 us -> 119 us (0.88); the launches traced: 134 us -> 119 us
  Pallas kernels: 132 us -> 118 us
    pallas_call x1, Pallas kernels: 130 us -> 116 us  [shards(): pl.pallas_call(kernel, out_shape=shapes, in_specs=[vmem] * 5 + [pl.BlockS...]
where the time goes in v2:
time: 119 us
  Pallas kernels  118 us (99%)
    pallas_call x1, Pallas kernels, shards(): pl.pallas_call(kernel, out_shape=shapes, in_specs=[vmem] * 5 + [pl.BlockS...  116 us

profile of v2, /device:TPU:1, one launch (start us, length us, event | category | flops | bytes accessed | tf_op | source)
XLA Modules:
  0.0 119.0 jit_solution(11119715540537735751)
XLA Ops:
  0.6 116.2 %shard_map.112 = (bf16[2,1,256,256]{3,2,1,0:T(8,128)(2,1)}, f32[1,2,256,256]{3,2,1,0:T(8,128)}, f32[1,2,256,256]{3,2,1,0:T(8,128)}) custom-call(bf16[1,256,256]{2,1,0:T(8,128)(2,1)} %grad_in.1, bf16[256,256]{1,0:T(8,128)(2,1)} %grad_last.1, bf16[1,2,2,256,256]{4,3,2,1,0:T(8,128)(2,1)} %support.1, bf16[1,2,2,256,256]{4,3,2,1,0:T(8,128)(2,1)} %preact.1, ...), custom_call_target="tpu_custom_call" | custom-call | tf_op jit(solution)/shard_map/pallas_call | solution.py:460
  116.8 2.1 %shard_map.113 = (bf16[2,1,256,256]{3,2,1,0:T(8,128)(2,1)}, f32[1,2,256,256]{3,2,1,0:T(8,128)}, f32[1,2,256,256]{3,2,1,0:T(8,128)}) custom-call(bf16[2,1,256,256]{3,2,1,0:T(8,128)(2,1)} %get-tuple-element.6.refs_0_, f32[1,2,256,256]{3,2,1,0:T(8,128)} %get-tuple-element.7.refs_1_, f32[1,2,256,256]{3,2,1,0:T(8,128)} %get-tuple-element.8.refs_2_), custom_call_target="tpu_custom_call" | custom-call | tf_op jit(solution)/shard_map/pallas_call | solution.py:517

commit v3 on v2

--- a/solution.py
+++ b/solution.py
@@ -16,15 +16,16 @@
 WIDTH = 256
 ROWS = 256
 LIST = 96
-RA = 64
+RA = 80
+PIECES = 4
 RC = TILE - RA
+PHASES = (16, 39, 48)
 ARRIVALS = (
-    (1, 0, 0), (1, 0, 1), (0, 7, 0), (0, 1, 0), (0, 7, 1), (0, 1, 1), (1, 7, 0), (1, 1, 0), (1, 7, 1), (1, 1, 1),
-    (0,),
-    (0, 6, 0), (0, 2, 0), (0, 6, 1), (0, 2, 1), (1, 6, 0), (1, 2, 0), (1, 6, 1), (1, 2, 1),
-    (7,), (0, 5, 0), (0, 3, 0), (1,),
-    (0, 5, 1), (0, 3, 1), (1, 5, 0), (1, 3, 0), (1, 5, 1), (1, 3, 1),
-    (6,), (0, 4, 0), (2,), (1, 4, 0), (0, 4, 1), (1, 4, 1), (5,), (3,), (4,),
+    (1, 0, 0), (0, 7, 0), (0, 1, 0), (1, 0, 1), (0, 7, 1), (0, 1, 1), (0, 7, 2), (0, 1, 2), (0, 7, 3), (0, 1, 3),
+    (1, 7, 0), (1, 1, 0), (0, 6, 0), (0, 2, 0), (0,), (1, 7, 1), (1, 1, 1), (0, 6, 1), (0, 2, 1), (0, 6, 2),
+    (0, 2, 2), (0, 6, 3), (0, 2, 3), (1, 6, 0), (1, 2, 0), (0, 5, 0), (0, 3, 0), (1, 6, 1), (1, 2, 1), (0, 5, 1),
+    (0, 3, 1), (7,), (0, 5, 2), (1,), (0, 3, 2), (0, 5, 3), (0, 3, 3), (1, 5, 0), (1, 3, 0), (0, 4, 0), (1, 3, 1),
+    (1, 5, 1), (0, 4, 1), (0, 4, 2), (6,), (2,), (0, 4, 3), (1, 4, 0), (1, 4, 1), (5,), (3,), (4,),
 )
 F32 = jnp.float32
 BF16 = jnp.bfloat16
@@ -32,14 +33,16 @@
 
 
 def kernel(
-    grad_in, grad_last, support, preact, weights, vals_hbm, row_in, col_in, count_in,
+    grad_hbm, last_hbm, support_hbm, preact_hbm, weights_hbm, vals_hbm, row_hbm, col_hbm, count_hbm,
+    hand_hbm, init_hbm, wg_hbm,
     hand_out, init_out, wg_out,
-    wg_acc, x_part, x_in, z_own, z_part, z_in, z_done, x_done,
+    row_in, col_in, count_in, grad_last, support, preact, weights, preact_dn, weights_dn, masked_dn, image_dn,
+    masked_in, wg_acc, x_part, x_in, z_own, z_part, z_in, done,
     vals, key_buf, tab_v, tab_s, need, need_at, run, near_adj, far_adj,
-    full, side, far, pick1, pick2a, pick3, pick2c, grad_buf, masked_buf, acc, handed,
-    vals_sem, tab_sem, need_send, need_recv, full_up, full_dn, full_recv,
+    full, side, far, pick1, pick2a, pick3, pick2c, grad_buf, masked_buf, acc,
+    in_sem, out_sem, vals_sem, tab_sem, need_send, need_recv, full_up, full_dn, full_recv,
     side_first, side_up, side_dn, side_recv, far_send, far_recv,
-    hand_send, hand_recv, sum_xs, sum_xr, sum_zs, sum_zr, fin_zs, fin_zr, fin_xs, fin_xr,
+    lend_send, lend_recv, own_send, own_recv, mask_send, mask_recv, next_up, next_dn, next_side, sum_xs, sum_xr, sum_zs, sum_zr, fin_zs, fin_zr, fin_xs, fin_xr,
 ):
     section = lax.axis_index("section")
     me = lax.axis_index("rows")
@@ -53,16 +56,32 @@
     across_z = [at(section, x, (z + d) % ZS) for d in range(1, ZS)]
     x_up, x_far, x_dn = across_x
     z_up, z_dn = across_z[0], across_z[-1]
-    s_up = at((section + 1) % SECTIONS, x, z)
-    s_dn = at((section + SECTIONS - 1) % SECTIONS, x, z)
-
-    for t in range(2):
-        pltpu.make_async_copy(vals_hbm.at[0, t], vals.at[t], vals_sem.at[t]).start()
+    above, below = (section + 1) % SECTIONS, (section + SECTIONS - 1) % SECTIONS
+    s_up, s_dn = at(above, x, z), at(below, x, z)
+    dn_side = at(below, (x + 1) % XS, z)
+    dn_z_up, dn_z_dn = at(below, x, (z + 1) % ZS), at(below, x, (z + ZS - 1) % ZS)
+    up_peers = [at(above, (x + XS - 1) % XS, z), at(above, x, (z + ZS - 1) % ZS), at(above, x, (z + 1) % ZS)]
 
     barrier = pltpu.get_barrier_semaphore()
-    peers = across_x + across_z + [s_up, s_dn]
+    peers = across_x + across_z + [s_up, s_dn, dn_side, dn_z_up, dn_z_dn] + up_peers
     for peer in peers:
         pl.semaphore_signal(barrier, inc=1, device_id=peer, device_id_type=MESH)
+
+    inputs = [
+        pltpu.make_async_copy(source, target, in_sem.at[n])
+        for n, (source, target) in enumerate((
+            (grad_hbm.at[0], grad_buf),
+            (preact_hbm.at[0], preact),
+            (weights_hbm.at[0], weights),
+            (col_hbm, col_in),
+            (row_hbm, row_in),
+            (count_hbm, count_in),
+            (support_hbm.at[0], support),
+            (last_hbm, grad_last),
+        ))
+    ] + [pltpu.make_async_copy(vals_hbm.at[0, t], vals.at[t], vals_sem.at[t]) for t in range(2)]
+    for copy in inputs:
+        copy.start()
 
     def remote(src, dst, send, recv, device):
         return pltpu.make_async_remote_copy(
@@ -73,13 +92,16 @@
     def tile(h):
         return pl.ds(h * TILE, TILE)
 
+    def piece(p):
+        return pl.ds(p * (ROWS // PIECES), ROWS // PIECES)
+
     def late(h):
         return pl.ds(h * RC, RC)
 
     def send_full(i, k, h, up):
         k_to = (k + (7 if up else 1)) % ZS
         return remote(
-            full.at[i, k, tile(h)], full.at[i, k_to, tile(h)],
+            full.at[i, k, piece(h)], full.at[i, k_to, piece(h)],
             (full_up if up else full_dn).at[k, h], full_recv.at[i, k_to, h], z_up if up else z_dn,
         )
 
@@ -108,8 +130,9 @@
         )
 
     def moves(c, k, h):
-        up = k in (0, 7, 6) or (k == 5 and h == 0)
-        dn = k in (0, 1, 2) or (k == 3 and h == 1)
+        first = h < (1 if c else PIECES // 2)
+        up = k in (0, 7, 6) or (k == 5 and first)
+        dn = k in (0, 1, 2) or (k == 3 and not first)
         return [way for way, goes in ((True, up), (False, dn)) if goes]
 
     need_copies = [
@@ -118,16 +141,16 @@
     ]
 
     def all_sends(i):
-        copies = [first_side(i, h) for h in range(2)]
+        copies = []
         for k in range(ZS):
-            for h in range(2):
-                for way in moves(0, k, h):
-                    copies += [send_full(i, k, h, way), send_side(i, k, h, way)]
+            if k:
+                copies += [send_full(i, k, p, way) for p in range(PIECES) for way in moves(0, k, p)]
+            copies += [send_side(i, k, h, way) for h in range(2) for way in moves(1, k, h)]
             copies += [send_far(i, k, n) for n in range(4)]
         return copies
 
-    def beta_of(layer):
-        depth = (2 * section + layer + 1).astype(F32)
+    def beta_of(place, layer):
+        depth = (2 * place + layer + 1).astype(F32)
         return jnp.log(BETA_SCALE / jnp.full((8, 128), depth, F32) + 1.0)[0:1, 0:1]
 
     def find_needs():
@@ -211,20 +234,17 @@
             sum_zs.at[w, d - 1], sum_zr.at[w, d - 1], across_z[d - 1],
         )
 
+    def fin_x(w, d):
+        return remote(
+            done.at[w, z, x], done.at[w, z, x],
+            fin_xs.at[w, d - 1], fin_xr.at[w, d - 1], across_x[d - 1],
+        )
+
     def fin_z(w, d):
         return remote(
-            z_done.at[w, z], z_done.at[w, z],
+            done.at[w, z], done.at[w, z],
             fin_zs.at[w, d - 1], fin_zr.at[w, d - 1], across_z[d - 1],
         )
-
-    def fin_x(w, d):
-        return remote(
-            x_done.at[w, x], x_done.at[w, x],
-            fin_xs.at[w, d - 1], fin_xr.at[w, d - 1], across_x[d - 1],
-        )
-
-    def got_fin(ref, w, d, place, recv, device):
-        remote(ref.at[w, place], ref.at[w, place], recv.at[w, d - 1], recv.at[w, d - 1], device).wait_recv()
 
     def scatter_x(w, total):
         x_part[w] = total.astype(BF16).reshape(XS, ROWS // XS, WIDTH)
@@ -245,29 +265,31 @@
         for d in range(1, ZS):
             sum_z(w, d).start()
 
-    def gather_z(w):
+    def gather_x(w):
         for d in range(1, ZS):
             sum_z(w, d).wait_recv()
         total = z_own[z]
         for d in range(1, ZS):
             total = total + z_in[w, d - 1].astype(F32)
-        z_done[w, z] = total.astype(BF16)
+        done[w, z, x] = total.astype(BF16)
+        for d in range(1, XS):
+            fin_x(w, d).start()
+
+    def gather_z(w):
+        for d in range(1, XS):
+            part = done.at[w, z, (x + XS - d) % XS]
+            remote(part, part, fin_xs.at[w, d - 1], fin_xr.at[w, d - 1], x_up).wait_recv()
         for d in range(1, ZS):
             fin_z(w, d).start()
 
-    def gather_x(w):
+    def finish_sum(w):
         for d in range(1, ZS):
-            got_fin(z_done, w, d, (z + ZS - d) % ZS, fin_zr, z_up)
+            part = done.at[w, (z + ZS - d) % ZS]
+            remote(part, part, fin_zs.at[w, d - 1], fin_zr.at[w, d - 1], z_up).wait_recv()
         for q in range(ZS):
-            x_done[w, x, 16 * (q // 2) : 16 * (q // 2) + 16, 128 * (q % 2) : 128 * (q % 2) + 128] = z_done[w, q]
-        for d in range(1, XS):
-            fin_x(w, d).start()
-
-    def finish_sum(w):
-        for d in range(1, XS):
-            got_fin(x_done, w, d, (x + XS - d) % XS, fin_xr, x_up)
-        for q in range(XS):
-            wg_out[0, w, q * (ROWS // XS) : (q + 1) * (ROWS // XS)] = x_done[w, q].astype(F32)
+            for r in range(XS):
+                top, left = r * (ROWS // XS) + 16 * (q // 2), 128 * (q % 2)
+                wg_out[0, w, top : top + 16, left : left + 128] = done[w, q, r].astype(F32)
         for d in range(1, XS):
             sum_x(w, d).wait_send()
             fin_x(w, d).wait_send()
@@ -275,44 +297,93 @@
             sum_z(w, d).wait_send()
             fin_z(w, d).wait_send()
 
-    find_needs()
+    lent = [
+        remote(preact.at[1, 1], preact_dn, lend_send.at[0], lend_recv.at[0], s_up),
+        remote(weights.at[1], weights_dn, lend_send.at[1], lend_recv.at[1], s_up),
+    ]
+
+    def give_own(h):
+        return remote(image_dn.at[tile(h)], full.at[2, 0, tile(h)], own_send.at[h], own_recv.at[h], s_dn)
+
+    def give_round(p, up):
+        return remote(
+            image_dn.at[piece(p)], full.at[2, 7 if up else 1, piece(p)],
+            (next_up if up else next_dn).at[p], full_recv.at[2, 7 if up else 1, p], dn_z_up if up else dn_z_dn,
+        )
+
+    def give_side(h):
+        return remote(
+            image_dn.at[pl.ds(h * TILE + RA, RC)], side.at[2, 0, late(h)],
+            next_side.at[h], side_recv.at[2, 0, h], dn_side,
+        )
+
+    give_masked = remote(masked_dn, masked_in, mask_send, mask_recv, s_dn)
+
+    def image_of(grad, live, beta, weight):
+        masked32 = jnp.where(live.astype(F32) > 0, grad, 0.0)
+        masked = masked32.astype(BF16)
+        turned = lax.dot_general(masked, weight, (((1,), (1,)), ((), ())), preferred_element_type=F32)
+        return masked, ((1.0 - beta) * masked32 + beta * turned).astype(BF16)
+
+    def leave(n):
+        source, target = (
+            (hand_out.at[0], hand_hbm.at[0]),
+            (init_out.at[0, 0], init_hbm.at[0, 0]),
+            (init_out.at[0, 1], init_hbm.at[0, 1]),
+            (wg_out.at[0, 1], wg_hbm.at[0, 1]),
+            (hand_out.at[1], hand_hbm.at[1]),
+            (wg_out.at[0, 0], wg_hbm.at[0, 0]),
+        )[n]
+        return pltpu.make_async_copy(source, target, out_sem.at[n])
 
     def step(i, carry):
         t = i // 2
         layer = 1 - i % 2
-        beta = beta_of(layer)
+        beta = beta_of(section, layer)
 
         @pl.when(i == 0)
         def _():
-            grad_buf[...] = grad_in[0]
-            pl.semaphore_wait(barrier, len(peers))
+            for copy in inputs[:3]:
+                copy.wait()
+
+        @pl.when(i != 2)
+        def _():
+            for h in range(2):
+                masked, image = image_of(
+                    grad_buf[tile(h)].astype(F32), preact[t, layer, tile(h)], beta, weights[layer]
+                )
+                masked_buf[tile(h)] = masked
+                full[i, 0, tile(h)] = image
+                if h == 0:
+                    @pl.when(i == 0)
+                    def _():
+                        pl.semaphore_wait(barrier, len(peers))
+
+                for p in range(h * PIECES // 2, (h + 1) * PIECES // 2):
+                    for way in (True, False):
+                        send_full(i, 0, p, way).start()
+                first_side(i, h).start()
+
+        @pl.when(i == 2)
+        def _():
+            for h in range(2):
+                give_own(h).wait_recv()
+            give_masked.wait_recv()
+            masked_buf[...] = masked_in[...]
+
+        @pl.when(i == 0)
+        def _():
+            for copy in lent:
+                copy.start()
+            for copy in inputs[3:]:
+                copy.wait()
+            find_needs()
             for copy in need_copies:
                 copy.start()
 
-        @pl.when(i == 2)
-        def _():
-            remote(grad_buf, handed, hand_send, hand_recv, s_dn).wait()
-            last = jnp.full((8, 128), section, I32)[0:1, 0:1] == SECTIONS - 1
-            grad_buf[...] = jnp.where(
-                last, grad_last[...].astype(F32), handed[...].astype(F32)
-            ).astype(BF16)
-
-        for h in range(2):
-            live = preact[0, t, layer, tile(h)].astype(F32) > 0
-            masked32 = jnp.where(live, grad_buf[tile(h)].astype(F32), 0.0)
-            masked = masked32.astype(BF16)
-            masked_buf[tile(h)] = masked
-            turned = lax.dot_general(
-                masked, weights[0, layer], (((1,), (1,)), ((), ())), preferred_element_type=F32
-            )
-            full[i, 0, tile(h)] = ((1.0 - beta) * masked32 + beta * turned).astype(BF16)
-            first_side(i, h).start()
-            for way in (True, False):
-                send_full(i, 0, h, way).start()
-
         shown = ALPHA * full[i, 0].astype(F32)
         term = beta * lax.dot_general(
-            support[0, t, layer], masked_buf[...], (((0,), (0,)), ((), ())),
+            support[t, layer], masked_buf[...], (((0,), (0,)), ((), ())),
             preferred_element_type=F32,
         )
 
@@ -332,10 +403,16 @@
         def _():
             init_out[0, t] += shown
 
+            @pl.when(t == 0)
+            def _():
+                leave(1).start()
+
+            @pl.when(t == 1)
+            def _():
+                leave(2).start()
+
         @pl.when(i == 0)
         def _():
-            for u in range(2):
-                pltpu.make_async_copy(vals_hbm.at[0, u], vals.at[u], vals_sem.at[u]).wait()
             build_adjacency(0)
             for copy in need_copies:
                 copy.wait()
@@ -381,6 +458,24 @@
         for n, arrival in enumerate(ARRIVALS):
             if len(arrival) == 1:
                 (k,) = arrival
+                if k == 4:
+                    for copy in all_sends(i):
+                        copy.wait_send()
+
+                    @pl.when(i != 2)
+                    def _():
+                        for copy in [first_side(i, h) for h in range(2)] + [
+                            send_full(i, 0, p, way) for p in range(PIECES) for way in (True, False)
+                        ]:
+                            copy.wait_send()
+
+                    @pl.when(i == 2)
+                    def _():
+                        for copy in [give_own(0), give_own(1), give_side(0), give_side(1), give_masked] + [
+                            give_round(p, way) for p in range(PIECES) for way in (True, False)
+                        ]:
+                            copy.wait_send()
+
                 for part in range(4):
                     send_far(i, k, part).wait_recv()
                 if k != 4:
@@ -389,7 +484,7 @@
                 c, k, h = arrival
                 if c == 0:
                     remote(
-                        full.at[i, k, tile(h)], full.at[i, k, tile(h)],
+                        full.at[i, k, piece(h)], full.at[i, k, piece(h)],
                         full_up.at[k, h], full_recv.at[i, k, h], z_up,
                     ).wait_recv()
                 else:
@@ -399,7 +494,8 @@
                     ).wait_recv()
                 for way in moves(c, k, h):
                     (send_side if c else send_full)(i, k, h, way).start()
-                if h == 1:
+                taken = [a[:2] for a in ARRIVALS[: n + 1]].count((c, k))
+                if taken == (2 if c else PIECES):
                     if c:
                         pass_side(k)
                     else:
@@ -408,30 +504,65 @@
 
             @pl.when(t == 1)
             def _():
-                if arrival == (0,):
+                if n == PHASES[0]:
                     scatter_z(layer)
-                elif arrival == (7,):
+                elif n == PHASES[1]:
+                    gather_x(layer)
+                elif n == PHASES[2]:
                     gather_z(layer)
-                elif arrival == (6,):
-                    gather_x(layer)
-
-        grad = ((1.0 - ALPHA) * (acc[...] + product(4, False))).astype(BF16)
-        grad_buf[...] = grad
-
-        @pl.when(i == 1)
-        def _():
-            remote(grad_buf, handed, hand_send, hand_recv, s_dn).start()
+
+            @pl.when(i == 3)
+            def _():
+                if n == PHASES[0]:
+                    finish_sum(1)
+                    leave(3).start()
+
+        for h in range(2):
+            spread = acc[tile(h)] + jnp.dot(
+                far_adj[t, 4, tile(h)], far[i, 4], preferred_element_type=F32
+            )
+            grad = ((1.0 - ALPHA) * spread).astype(BF16)
+            grad_buf[tile(h)] = grad
+
+            @pl.when(i == 1)
+            def _():
+                if h == 0:
+                    for copy in lent:
+                        copy.wait()
+                wraps = jnp.full((8, 128), section, I32)[0:1, 0:1] == 0
+                masked, image = image_of(
+                    jnp.where(wraps, grad_last[tile(h)].astype(F32), grad.astype(F32)),
+                    preact_dn[tile(h)], beta_of(below, 1), weights_dn[...],
+                )
+                masked_dn[tile(h)] = masked
+                image_dn[tile(h)] = image
+                for p in range(h * PIECES // 2, (h + 1) * PIECES // 2):
+                    for way in (True, False):
+                        give_round(p, way).start()
+                give_side(h).start()
+                give_own(h).start()
+                if h == 1:
+                    give_masked.start()
 
         @pl.when(layer == 0)
         def _():
-            hand_out[t, 0] = grad
-
-        @pl.when(t == 1)
-        def _():
-            finish_sum(layer)
-
-        for copy in all_sends(i):
-            copy.wait_send()
+            hand_out[t, 0] = grad_buf[...]
+
+            @pl.when(t == 0)
+            def _():
+                leave(0).start()
+
+            @pl.when(t == 1)
+            def _():
+                leave(4).start()
+
+        @pl.when(i == 3)
+        def _():
+            finish_sum(0)
+            leave(5).start()
+            for n in range(6):
+                leave(n).wait()
+
         return carry
 
     lax.fori_loop(0, 4, step, 0)
@@ -451,7 +582,7 @@
 
 
 def shards(grad_in, grad_last, support, preact, weights, tile_vals, tile_row, tile_col, tile_count):
-    vmem = pl.BlockSpec(memory_space=pltpu.VMEM)
+    anywhere = pl.BlockSpec(memory_space=pl.ANY)
     shapes = (
         jax.ShapeDtypeStruct((2, 1, ROWS, WIDTH), BF16),
         jax.ShapeDtypeStruct((1, 2, ROWS, WIDTH), F32),
@@ -460,18 +591,29 @@
     results = pl.pallas_call(
         kernel,
         out_shape=shapes,
-        in_specs=[vmem] * 5
-        + [pl.BlockSpec(memory_space=pl.ANY), vmem, vmem, vmem],
-        out_specs=(vmem, vmem, vmem),
-        scratch_shapes=[
+        in_specs=[anywhere] * 9,
+        out_specs=(anywhere,) * 3,
+        scratch_shapes=[pltpu.VMEM(s.shape, s.dtype) for s in shapes]
+        + [
+            pltpu.VMEM((1, 2, LIST), I32),
+            pltpu.VMEM((1, 2, LIST), I32),
+            pltpu.VMEM((1, 1, 2), I32),
+            pltpu.VMEM((ROWS, WIDTH), BF16),
+            pltpu.VMEM((2, 2, ROWS, WIDTH), BF16),
+            pltpu.VMEM((2, 2, ROWS, WIDTH), BF16),
+            pltpu.VMEM((2, WIDTH, WIDTH), BF16),
+            pltpu.VMEM((ROWS, WIDTH), BF16),
+            pltpu.VMEM((WIDTH, WIDTH), BF16),
+            pltpu.VMEM((ROWS, WIDTH), BF16),
+            pltpu.VMEM((ROWS, WIDTH), BF16),
+            pltpu.VMEM((ROWS, WIDTH), BF16),
             pltpu.VMEM((2, WIDTH, WIDTH), F32),
             pltpu.VMEM((2, XS, ROWS // XS, WIDTH), BF16),
             pltpu.VMEM((2, XS - 1, ROWS // XS, WIDTH), BF16),
             pltpu.VMEM((ZS, 16, 128), F32),
             pltpu.VMEM((2, ZS, 16, 128), BF16),
             pltpu.VMEM((2, ZS - 1, 16, 128), BF16),
-            pltpu.VMEM((2, ZS, 16, 128), BF16),
-            pltpu.VMEM((2, XS, ROWS // XS, WIDTH), BF16),
+            pltpu.VMEM((2, ZS, XS, 16, 128), BF16),
             pltpu.VMEM((2, LIST, TILE, TILE), BF16),
             pltpu.VMEM((8, 128), I32),
             pltpu.VMEM((8, 128), I32),
@@ -491,29 +633,36 @@
             pltpu.VMEM((ROWS, WIDTH), BF16),
             pltpu.VMEM((ROWS, WIDTH), BF16),
             pltpu.VMEM((ROWS, WIDTH), F32),
-            pltpu.VMEM((ROWS, WIDTH), BF16),
+            pltpu.SemaphoreType.DMA((8,)),
+            pltpu.SemaphoreType.DMA((6,)),
             pltpu.SemaphoreType.DMA((2,)),
             pltpu.SemaphoreType.DMA,
             pltpu.SemaphoreType.DMA((3,)),
             pltpu.SemaphoreType.DMA((3,)),
-            pltpu.SemaphoreType.DMA((ZS, 2)),
-            pltpu.SemaphoreType.DMA((ZS, 2)),
-            pltpu.SemaphoreType.DMA((4, ZS, 2)),
+            pltpu.SemaphoreType.DMA((ZS, PIECES)),
+            pltpu.SemaphoreType.DMA((ZS, PIECES)),
+            pltpu.SemaphoreType.DMA((4, ZS, PIECES)),
             pltpu.SemaphoreType.DMA((2,)),
             pltpu.SemaphoreType.DMA((ZS, 2)),
             pltpu.SemaphoreType.DMA((ZS, 2)),
             pltpu.SemaphoreType.DMA((4, ZS, 2)),
             pltpu.SemaphoreType.DMA((4, ZS)),
             pltpu.SemaphoreType.DMA((4, 4, ZS)),
+            pltpu.SemaphoreType.DMA((2,)),
+            pltpu.SemaphoreType.DMA((2,)),
+            pltpu.SemaphoreType.DMA((2,)),
+            pltpu.SemaphoreType.DMA((2,)),
             pltpu.SemaphoreType.DMA,
             pltpu.SemaphoreType.DMA,
+            pltpu.SemaphoreType.DMA((PIECES,)),
+            pltpu.SemaphoreType.DMA((PIECES,)),
+            pltpu.SemaphoreType.DMA((2,)),
         ]
         + [pltpu.SemaphoreType.DMA((2, n - 1)) for n in (XS, XS, ZS, ZS, ZS, ZS, XS, XS)],
         compiler_params=pltpu.CompilerParams(
             collective_id=0, has_side_effects=True, vmem_limit_bytes=60 * 1024 * 1024
         ),
     )(grad_in, grad_last, support, preact, weights, tile_vals, tile_row, tile_col, jnp.swapaxes(tile_count, 1, 2))
-    anywhere = pl.BlockSpec(memory_space=pl.ANY)
     return pl.pallas_call(
         write_results,
         out_shape=shapes,

time: 119 us -> 117 us (0.983)
  Pallas kernels: 118 us -> 116 us
    pallas_call x1, Pallas kernels: 116 us -> 114 us  [shards(): pl.pallas_call(kernel, out_shape=shapes, in_specs=[anywhere] * 9, out_spe...]
where the time goes in v3:
time: 117 us
  Pallas kernels  116 us (99%)
    pallas_call x1, Pallas kernels, shards(): pl.pallas_call(kernel, out_shape=shapes, in_specs=[anywhere] * 9, out_spe...  114 us

profile of v3, /device:TPU:1, one launch (start us, length us, event | category | flops | bytes accessed | tf_op | source)
XLA Modules:
  0.0 117.1 jit_solution(7266165002579989853)
XLA Ops:
  0.6 114.3 %shard_map.112 = (bf16[2,1,256,256]{3,2,1,0:T(8,128)(2,1)}, f32[1,2,256,256]{3,2,1,0:T(8,128)}, f32[1,2,256,256]{3,2,1,0:T(8,128)}) custom-call(bf16[1,256,256]{2,1,0:T(8,128)(2,1)} %grad_hbm.1, bf16[256,256]{1,0:T(8,128)(2,1)} %last_hbm.1, bf16[1,2,2,256,256]{4,3,2,1,0:T(8,128)(2,1)} %support_hbm.1, bf16[1,2,2,256,256]{4,3,2,1,0:T(8,128)(2,1)} %preact_hbm.1, ...), custom_call_target="tpu_custom_call" | custom-call | tf_op jit(solution)/shard_map/pallas_call | solution.py:591
  115.0 2.1 %shard_map.113 = (bf16[2,1,256,256]{3,2,1,0:T(8,128)(2,1)}, f32[1,2,256,256]{3,2,1,0:T(8,128)}, f32[1,2,256,256]{3,2,1,0:T(8,128)}) custom-call(bf16[2,1,256,256]{3,2,1,0:T(8,128)(2,1)} %get-tuple-element.6.refs_0_, f32[1,2,256,256]{3,2,1,0:T(8,128)} %get-tuple-element.7.refs_1_, f32[1,2,256,256]{3,2,1,0:T(8,128)} %get-tuple-element.8.refs_2_), custom_call_target="tpu_custom_call" | custom-call | tf_op jit(solution)/shard_map/pallas_call | solution.py:666

commit v4 on v3

--- a/solution.py
+++ b/solution.py
@@ -16,16 +16,17 @@
 WIDTH = 256
 ROWS = 256
 LIST = 96
-RA = 80
+RA = 64
 PIECES = 4
 RC = TILE - RA
-PHASES = (16, 39, 48)
+LATE_TERM = 36
+PHASES = (9, 19, 28, 42, 47)
 ARRIVALS = (
     (1, 0, 0), (0, 7, 0), (0, 1, 0), (1, 0, 1), (0, 7, 1), (0, 1, 1), (0, 7, 2), (0, 1, 2), (0, 7, 3), (0, 1, 3),
-    (1, 7, 0), (1, 1, 0), (0, 6, 0), (0, 2, 0), (0,), (1, 7, 1), (1, 1, 1), (0, 6, 1), (0, 2, 1), (0, 6, 2),
-    (0, 2, 2), (0, 6, 3), (0, 2, 3), (1, 6, 0), (1, 2, 0), (0, 5, 0), (0, 3, 0), (1, 6, 1), (1, 2, 1), (0, 5, 1),
-    (0, 3, 1), (7,), (0, 5, 2), (1,), (0, 3, 2), (0, 5, 3), (0, 3, 3), (1, 5, 0), (1, 3, 0), (0, 4, 0), (1, 3, 1),
-    (1, 5, 1), (0, 4, 1), (0, 4, 2), (6,), (2,), (0, 4, 3), (1, 4, 0), (1, 4, 1), (5,), (3,), (4,),
+    (1, 7, 0), (1, 1, 0), (0, 6, 0), (0, 2, 0), (1, 7, 1), (1, 1, 1), (0, 6, 1), (0, 2, 1), (0, 6, 2), (0, 2, 2),
+    (0, 6, 3), (0, 2, 3), (1, 6, 0), (1, 2, 0), (0,), (0, 5, 0), (0, 3, 0), (1, 6, 1), (1, 2, 1), (0, 5, 1),
+    (0, 3, 1), (0, 5, 2), (0, 3, 2), (0, 5, 3), (0, 3, 3), (1, 5, 0), (1, 3, 0), (0, 4, 0), (1, 3, 1), (1, 5, 1),
+    (7,), (1,), (0, 4, 1), (0, 4, 2), (0, 4, 3), (1, 4, 0), (1, 4, 1), (6,), (2,), (5,), (3,), (4,),
 )
 F32 = jnp.float32
 BF16 = jnp.bfloat16
@@ -37,12 +38,12 @@
     hand_hbm, init_hbm, wg_hbm,
     hand_out, init_out, wg_out,
     row_in, col_in, count_in, grad_last, support, preact, weights, preact_dn, weights_dn, masked_dn, image_dn,
-    masked_in, wg_acc, x_part, x_in, z_own, z_part, z_in, done,
+    masked_in, wg_acc, x_part, x_in, z_own, z_part, z_in, done, zz_part, zz_in, xx_own, xx_part, xx_in,
     vals, key_buf, tab_v, tab_s, need, need_at, run, near_adj, far_adj,
     full, side, far, pick1, pick2a, pick3, pick2c, grad_buf, masked_buf, acc,
     in_sem, out_sem, vals_sem, tab_sem, need_send, need_recv, full_up, full_dn, full_recv,
     side_first, side_up, side_dn, side_recv, far_send, far_recv,
-    lend_send, lend_recv, own_send, own_recv, mask_send, mask_recv, next_up, next_dn, next_side, sum_xs, sum_xr, sum_zs, sum_zr, fin_zs, fin_zr, fin_xs, fin_xr,
+    lend_send, lend_recv, own_send, own_recv, mask_send, mask_recv, next_up, next_dn, next_side, zz_send, zz_recv, xx_send, xx_recv, sum_xs, sum_xr, sum_zs, sum_zr, fin_zs, fin_zr, fin_xs, fin_xr,
 ):
     section = lax.axis_index("section")
     me = lax.axis_index("rows")
@@ -265,12 +266,47 @@
         for d in range(1, ZS):
             sum_z(w, d).start()
 
+    def sum_zz(d):
+        return remote(
+            zz_part.at[(z + d) % ZS], zz_in.at[d - 1], zz_send.at[d - 1], zz_recv.at[d - 1], across_z[d - 1]
+        )
+
+    def sum_xx(d):
+        return remote(
+            xx_part.at[(x + d) % XS], xx_in.at[d - 1], xx_send.at[d - 1], xx_recv.at[d - 1], across_x[d - 1]
+        )
+
+    def scatter_zz():
+        zz_part[...] = wg_acc[1].astype(BF16).reshape(ZS, ROWS // ZS, WIDTH)
+        for d in range(1, ZS):
+            sum_zz(d).start()
+
+    def scatter_xx():
+        for d in range(1, ZS):
+            sum_zz(d).wait()
+        total = wg_acc[1, pl.ds(z * (ROWS // ZS), ROWS // ZS)]
+        for d in range(1, ZS):
+            total = total + zz_in[d - 1].astype(F32)
+        for r in range(XS):
+            part = total[16 * (r // 2) : 16 * (r // 2) + 16, 128 * (r % 2) : 128 * (r % 2) + 128]
+            xx_own[r] = part
+            xx_part[r] = part.astype(BF16)
+        for d in range(1, XS):
+            sum_xx(d).start()
+
     def gather_x(w):
-        for d in range(1, ZS):
-            sum_z(w, d).wait_recv()
-        total = z_own[z]
-        for d in range(1, ZS):
-            total = total + z_in[w, d - 1].astype(F32)
+        if w:
+            for d in range(1, XS):
+                sum_xx(d).wait()
+            total = xx_own[x]
+            for d in range(1, XS):
+                total = total + xx_in[d - 1].astype(F32)
+        else:
+            for d in range(1, ZS):
+                sum_z(w, d).wait_recv()
+            total = z_own[z]
+            for d in range(1, ZS):
+                total = total + z_in[w, d - 1].astype(F32)
         done[w, z, x] = total.astype(BF16)
         for d in range(1, XS):
             fin_x(w, d).start()
@@ -288,14 +324,19 @@
             remote(part, part, fin_zs.at[w, d - 1], fin_zr.at[w, d - 1], z_up).wait_recv()
         for q in range(ZS):
             for r in range(XS):
-                top, left = r * (ROWS // XS) + 16 * (q // 2), 128 * (q % 2)
+                if w:
+                    top, left = q * (ROWS // ZS) + 16 * (r // 2), 128 * (r % 2)
+                else:
+                    top, left = r * (ROWS // XS) + 16 * (q // 2), 128 * (q % 2)
                 wg_out[0, w, top : top + 16, left : left + 128] = done[w, q, r].astype(F32)
         for d in range(1, XS):
-            sum_x(w, d).wait_send()
             fin_x(w, d).wait_send()
+            if w == 0:
+                sum_x(w, d).wait_send()
         for d in range(1, ZS):
-            sum_z(w, d).wait_send()
             fin_z(w, d).wait_send()
+            if w == 0:
+                sum_z(w, d).wait_send()
 
     lent = [
         remote(preact.at[1, 1], preact_dn, lend_send.at[0], lend_recv.at[0], s_up),
@@ -368,32 +409,41 @@
         def _():
             for h in range(2):
                 give_own(h).wait_recv()
-            give_masked.wait_recv()
-            masked_buf[...] = masked_in[...]
 
         @pl.when(i == 0)
         def _():
             for copy in lent:
                 copy.start()
-            for copy in inputs[3:]:
+            for copy in inputs[3:6]:
                 copy.wait()
             find_needs()
             for copy in need_copies:
                 copy.start()
+            for copy in inputs[6:]:
+                copy.wait()
 
         shown = ALPHA * full[i, 0].astype(F32)
-        term = beta * lax.dot_general(
-            support[t, layer], masked_buf[...], (((0,), (0,)), ((), ())),
-            preferred_element_type=F32,
-        )
-
-        @pl.when(t == 0)
-        def _():
-            wg_acc[layer] = term
-
-        @pl.when(t == 1)
-        def _():
-            scatter_x(layer, wg_acc[layer] + term)
+        def weight_term():
+            term = beta * lax.dot_general(
+                support[t, layer], masked_buf[...], (((0,), (0,)), ((), ())),
+                preferred_element_type=F32,
+            )
+
+            @pl.when(t == 0)
+            def _():
+                wg_acc[layer] = term
+
+            @pl.when(i == 2)
+            def _():
+                wg_acc[1] += term
+
+            @pl.when(i == 3)
+            def _():
+                scatter_x(0, wg_acc[0] + term)
+
+        @pl.when(i != 2)
+        def _():
+            weight_term()
 
         @pl.when(layer == 1)
         def _():
@@ -502,20 +552,31 @@
                         pass_full(k)
                         acc[...] += product(k, True)
 
-            @pl.when(t == 1)
+            if n == LATE_TERM:
+                @pl.when(i == 2)
+                def _():
+                    give_masked.wait_recv()
+                    masked_buf[...] = masked_in[...]
+                    weight_term()
+
+            @pl.when(i == 2)
+            def _():
+                if n == PHASES[3]:
+                    scatter_zz()
+
+            @pl.when(i == 3)
             def _():
                 if n == PHASES[0]:
-                    scatter_z(layer)
+                    scatter_xx()
                 elif n == PHASES[1]:
-                    gather_x(layer)
+                    scatter_z(0)
                 elif n == PHASES[2]:
-                    gather_z(layer)
-
-            @pl.when(i == 3)
-            def _():
-                if n == PHASES[0]:
-                    finish_sum(1)
-                    leave(3).start()
+                    gather_x(1)
+                elif n == PHASES[3]:
+                    gather_z(1)
+                    gather_x(0)
+                elif n == PHASES[4]:
+                    gather_z(0)
 
         for h in range(2):
             spread = acc[tile(h)] + jnp.dot(
@@ -558,6 +619,8 @@
 
         @pl.when(i == 3)
         def _():
+            finish_sum(1)
+            leave(3).start()
             finish_sum(0)
             leave(5).start()
             for n in range(6):
@@ -614,6 +677,11 @@
             pltpu.VMEM((2, ZS, 16, 128), BF16),
             pltpu.VMEM((2, ZS - 1, 16, 128), BF16),
             pltpu.VMEM((2, ZS, XS, 16, 128), BF16),
+            pltpu.VMEM((ZS, ROWS // ZS, WIDTH), BF16),
+            pltpu.VMEM((ZS - 1, ROWS // ZS, WIDTH), BF16),
+            pltpu.VMEM((XS, 16, 128), F32),
+            pltpu.VMEM((XS, 16, 128), BF16),
+            pltpu.VMEM((XS - 1, 16, 128), BF16),
             pltpu.VMEM((2, LIST, TILE, TILE), BF16),
             pltpu.VMEM((8, 128), I32),
             pltpu.VMEM((8, 128), I32),
@@ -657,6 +725,10 @@
             pltpu.SemaphoreType.DMA((PIECES,)),
             pltpu.SemaphoreType.DMA((PIECES,)),
             pltpu.SemaphoreType.DMA((2,)),
+            pltpu.SemaphoreType.DMA((ZS - 1,)),
+            pltpu.SemaphoreType.DMA((ZS - 1,)),
+            pltpu.SemaphoreType.DMA((XS - 1,)),
+            pltpu.SemaphoreType.DMA((XS - 1,)),
         ]
         + [pltpu.SemaphoreType.DMA((2, n - 1)) for n in (XS, XS, ZS, ZS, ZS, ZS, XS, XS)],
         compiler_params=pltpu.CompilerParams(

time: 117 us -> 116 us (level)
  no operation moved by 1% of the time
where the time goes in v4:
time: 116 us
  Pallas kernels  116 us (100%)
    pallas_call x1, Pallas kernels, shards(): pl.pallas_call(kernel, out_shape=shapes, in_specs=[anywhere] * 9, out_spe...  113 us

profile of v4, /device:TPU:1, one launch (start us, length us, event | category | flops | bytes accessed | tf_op | source)
XLA Modules:
  0.0 116.3 jit_solution(7752738479963659756)
XLA Ops:
  0.6 113.5 %shard_map.112 = (bf16[2,1,256,256]{3,2,1,0:T(8,128)(2,1)}, f32[1,2,256,256]{3,2,1,0:T(8,128)}, f32[1,2,256,256]{3,2,1,0:T(8,128)}) custom-call(bf16[1,256,256]{2,1,0:T(8,128)(2,1)} %grad_hbm.1, bf16[256,256]{1,0:T(8,128)(2,1)} %last_hbm.1, bf16[1,2,2,256,256]{4,3,2,1,0:T(8,128)(2,1)} %support_hbm.1, bf16[1,2,2,256,256]{4,3,2,1,0:T(8,128)(2,1)} %preact_hbm.1, ...), custom_call_target="tpu_custom_call" | custom-call | tf_op jit(solution)/shard_map/pallas_call | solution.py:654
  114.1 2.1 %shard_map.113 = (bf16[2,1,256,256]{3,2,1,0:T(8,128)(2,1)}, f32[1,2,256,256]{3,2,1,0:T(8,128)}, f32[1,2,256,256]{3,2,1,0:T(8,128)}) custom-call(bf16[2,1,256,256]{3,2,1,0:T(8,128)(2,1)} %get-tuple-element.6.refs_0_, f32[1,2,256,256]{3,2,1,0:T(8,128)} %get-tuple-element.7.refs_1_, f32[1,2,256,256]{3,2,1,0:T(8,128)} %get-tuple-element.8.refs_2_), custom_call_target="tpu_custom_call" | custom-call | tf_op jit(solution)/shard_map/pallas_call | solution.py:738

commit v5 on v4

--- a/solution.py
+++ b/solution.py
@@ -476,7 +476,7 @@
 
         def pass_full(k):
             for table, q, n, target, rows in (
-                (from_dn, 1, 0, pick1, TILE), (from_far, 2, 1, pick2a, RA), (from_up, 3, 2, pick3, RA)
+                (from_far, 2, 1, pick2a, RA), (from_dn, 1, 0, pick1, TILE), (from_up, 3, 2, pick3, RA)
             ):
                 first, second = chosen(table, q, k)
                 target[k] = (

time: 116 us -> 116 us (level)
  no operation moved by 1% of the time
where the time goes in v5:
time: 116 us
  Pallas kernels  116 us (100%)
    pallas_call x1, Pallas kernels, shards(): pl.pallas_call(kernel, out_shape=shapes, in_specs=[anywhere] * 9, out_spe...  114 us

profile of v5, /device:TPU:1, one launch (start us, length us, event | category | flops | bytes accessed | tf_op | source)
XLA Modules:
  0.0 116.3 jit_solution(3020578582650701255)
XLA Ops:
  0.6 113.5 %shard_map.112 = (bf16[2,1,256,256]{3,2,1,0:T(8,128)(2,1)}, f32[1,2,256,256]{3,2,1,0:T(8,128)}, f32[1,2,256,256]{3,2,1,0:T(8,128)}) custom-call(bf16[1,256,256]{2,1,0:T(8,128)(2,1)} %grad_hbm.1, bf16[256,256]{1,0:T(8,128)(2,1)} %last_hbm.1, bf16[1,2,2,256,256]{4,3,2,1,0:T(8,128)(2,1)} %support_hbm.1, bf16[1,2,2,256,256]{4,3,2,1,0:T(8,128)(2,1)} %preact_hbm.1, ...), custom_call_target="tpu_custom_call" | custom-call | tf_op jit(solution)/shard_map/pallas_call | solution.py:654
  114.1 2.1 %shard_map.113 = (bf16[2,1,256,256]{3,2,1,0:T(8,128)(2,1)}, f32[1,2,256,256]{3,2,1,0:T(8,128)}, f32[1,2,256,256]{3,2,1,0:T(8,128)}) custom-call(bf16[2,1,256,256]{3,2,1,0:T(8,128)(2,1)} %get-tuple-element.6.refs_0_, f32[1,2,256,256]{3,2,1,0:T(8,128)} %get-tuple-element.7.refs_1_, f32[1,2,256,256]{3,2,1,0:T(8,128)} %get-tuple-element.8.refs_2_), custom_call_target="tpu_custom_call" | custom-call | tf_op jit(solution)/shard_map/pallas_call | solution.py:738
